TPU v7x, 512 devices: a whole 4x4x16 slice. The times are simulated.
512 devices in a mesh: seq: 128 (over y, x, z_hi, core), head: 4 (over z_lo).
Axes of the slice: x: 4, y: 4, z: 16 (z_hi: 4, z_lo: 4; z = z_hi * 4 + z_lo), core: 2. Of those that a mesh axis runs over, the one named last changes fastest.
Arguments:
- tokens: int32 [16384], P('seq'), may hold values from 0 to 11
- residual_in: bfloat16 [16384, 2048], P('seq'), may hold values from -5 to 5
- pairing: int32 [2048], replicated, may hold values from 0 to 2047, as said below
- embedding: bfloat16 [12, 2048], replicated, may hold values from -5 to 5
- x_weight: bfloat16 [2048, 2048], P(None, 'head'), may hold values from -0.125 to 0.125
- bc_weight: bfloat16 [2048, 256], replicated, may hold values from -0.03125 to 0.03125
- dt_weight: bfloat16 [2048, 32], P(None, 'head'), may hold values from -0.125 to 0.125
- dt_bias: float32 [32], P('head'), may hold values from -8 to -1
- decay_rate: float32 [32], P('head'), may hold values from 0 to 1
- skip_gain: float32 [32], P('head'), may hold values from 0.5 to 1.5
- cotangent: bfloat16 [16384, 2048], P('seq', 'head'), may hold values from -6 to 6
Outputs:
- input_grad: float32 [2048, 16384], P('head', 'seq')
- saliency: float32 [16384], P('seq')
Inputs may be any that keep to these rules, and one draw needn't show every extreme that they name: pairing[pairing[d]] = d and pairing[d] != d.
All inputs are finite; a program needn't handle non-finite values.
Results may differ from a plain program's by a relative error of at most 0.0056.
Values sent between devices are 32-bit elements; how exact they have to be, the bound alone decides.
A program may use at most 64 MiB of HBM per device.

v0:
```python
import math

import jax
import jax.numpy as jnp
from jax import lax
from jax.sharding import PartitionSpec as P

GROUP = 128


highest = lax.Precision.HIGHEST


def shifted(value, axis, steps):
    count = lax.axis_size(axis)
    first, last = (max(0, -steps), min(count, count - steps))
    return lax.ppermute(value, axis, [(source, source + steps) for source in range(first, last)])


def strides(pre, dt_bias, decay_rate):
    stride = jax.nn.softplus(pre + dt_bias[None, :])
    return (stride, -decay_rate[None, :] * stride)


def group_scan(inputs, writer, reader, pre, dt_bias, decay_rate, skip_gain, start):
    stride, log_decay = strides(pre, dt_bias, decay_rate)
    length = inputs.shape[0]
    blocks = length // GROUP
    heads = inputs.shape[1]
    headdim = inputs.shape[2]
    state_dim = writer.shape[1]
    causal = (jnp.arange(GROUP)[:, None] >= jnp.arange(GROUP)[None, :])[:, :, None]

    def advance(state, pieces):
        in_block, write_block, read_block, stride_block, decay_block = pieces
        running = jnp.cumsum(decay_block, axis=0)
        from_state = jnp.exp(running)[:, :, None] * jnp.einsum(
            "hpn,qn->qhp", state, read_block, precision=highest
        )
        scores = jnp.einsum("qn,sn->qs", read_block, write_block, precision=highest)
        spread = running[:, None, :] - running[None, :, :]
        weights = (
            jnp.exp(jnp.where(causal, spread, -jnp.inf))
            * scores[:, :, None]
            * stride_block[None, :, :]
        )
        within = jnp.einsum("qsh,shp->qhp", weights, in_block, precision=highest)
        result = from_state + within + skip_gain[None, :, None] * in_block
        last_sum = running[-1]
        carry_weight = jnp.exp(last_sum[None, :] - running) * stride_block
        state = jnp.exp(last_sum)[:, None, None] * state + jnp.einsum(
            "sh,shp,sn->hpn", carry_weight, in_block, write_block, precision=highest
        )
        return (state, result)

    pieces = (
        inputs.reshape(blocks, GROUP, heads, headdim),
        writer.reshape(blocks, GROUP, state_dim),
        reader.reshape(blocks, GROUP, state_dim),
        stride.reshape(blocks, GROUP, heads),
        log_decay.reshape(blocks, GROUP, heads),
    )
    final, outputs = lax.scan(jax.checkpoint(advance), start, pieces)
    return (outputs.reshape(length, heads, headdim), final)


def combine(earlier, later):
    joined = []
    joined.append(earlier[0] * later[0])
    joined.append(later[0][:, None, None] * earlier[1] + later[1])
    return tuple(joined)


def doubling(values, identity, reverse, mover):
    count = lax.axis_size("seq")
    place = lax.axis_index("seq")
    direction = -1 if reverse else 1

    def fetch(current, distance):
        offset = direction * distance
        arrived = mover(current, offset)
        anchor_index = place - offset
        inside = (anchor_index >= 0) & (anchor_index < count)
        return tuple((jnp.where(inside, got, blank) for got, blank in zip(arrived, identity)))

    current = fetch(values, 1)
    distance = 1
    while distance < count:
        current = combine(fetch(current, distance), current)
        distance = distance * 2
    return current


def shards(
    tokens,
    residual_in,
    pairing,
    embedding,
    x_weight,
    bc_weight,
    dt_weight,
    dt_bias,
    decay_rate,
    skip_gain,
    cotangent,
):
    length = tokens.shape[0]
    heads = dt_weight.shape[1]
    headdim = x_weight.shape[1] // heads
    state_dim = bc_weight.shape[1] // 2
    width = x_weight.shape[0]
    vocab_ids = jnp.arange(embedding.shape[0], dtype=jnp.int32)
    one_hot = (tokens[:, None] == vocab_ids[None, :]).astype(jnp.bfloat16)
    layer_in = (
        jnp.dot(one_hot, embedding, preferred_element_type=jnp.float32)
        + residual_in.astype(jnp.float32)
    ).astype(jnp.bfloat16)
    upstream = cotangent.astype(jnp.float32).reshape(length, heads, headdim)
    paired = jnp.take(layer_in, pairing, axis=1)

    def project(source):
        inputs = jnp.dot(source, x_weight, preferred_element_type=jnp.float32).reshape(
            length, heads, headdim
        )
        mixed = jnp.dot(source, bc_weight, preferred_element_type=jnp.float32)
        pre = jnp.dot(source, dt_weight, preferred_element_type=jnp.float32)
        return (inputs, mixed, pre)

    def summaries(projected, upper):
        inputs, mixed, pre = projected
        stride, log_decay = strides(pre, dt_bias, decay_rate)
        running = jnp.cumsum(log_decay, axis=0)
        last_sum = running[-1]
        carry_weight = jnp.exp(last_sum[None, :] - running) * stride
        block_end = jnp.einsum(
            "sh,shp,sn->hpn", carry_weight, inputs, mixed[:, :state_dim], precision=highest
        )
        direct = jnp.einsum(
            "th,thp,tn->hpn", jnp.exp(running), upper, mixed[:, state_dim:], precision=highest
        )
        return (jnp.exp(last_sum), block_end, direct)

    forward_proj = project(layer_in)
    reverse_proj = project(jnp.flip(paired, 0))
    reverse_upper = jnp.flip(upstream, 0)
    factor_f, end_f, direct_f = summaries(forward_proj, upstream)
    factor_r, end_r, direct_r = summaries(reverse_proj, reverse_upper)
    blank = (jnp.ones((heads,), jnp.float32), jnp.zeros((heads, headdim, state_dim), jnp.float32))

    def move_single(current, offset):
        return shifted(current, "seq", offset)

    entry_f = doubling((factor_f, end_f), blank, False, move_single)[1]
    entry_r = doubling((factor_r, end_r), blank, True, move_single)[1]
    later_f = doubling((factor_f, direct_f), blank, True, move_single)[1]
    later_r = doubling((factor_r, direct_r), blank, False, move_single)[1]

    def pulled(projected, upper, entry, later):
        inputs, mixed, pre = projected

        def mixer(inputs, writer, reader, pre):
            return group_scan(inputs, writer, reader, pre, dt_bias, decay_rate, skip_gain, entry)

        outputs, pull = jax.vjp(mixer, inputs, mixed[:, :state_dim], mixed[:, state_dim:], pre)
        d_inputs, d_writer, d_reader, d_pre = pull((upper, later))
        return (
            d_inputs.reshape(length, heads * headdim).astype(jnp.bfloat16),
            d_pre.astype(jnp.bfloat16),
            jnp.concatenate([d_writer, d_reader], axis=1),
        )

    grads_f = pulled(forward_proj, upstream, entry_f, later_f)
    grads_r = tuple(
        (jnp.flip(member, 0) for member in pulled(reverse_proj, reverse_upper, entry_r, later_r))
    )
    rows_here = width // lax.axis_size("head")
    sources = (
        (x_weight, dt_weight, bc_weight, grads_f),
        (
            jnp.take(x_weight, pairing, axis=0),
            jnp.take(dt_weight, pairing, axis=0),
            jnp.take(bc_weight, pairing, axis=0),
            grads_r,
        ),
    )
    total = jnp.zeros((width, length), jnp.float32)
    for x_rows, dt_rows, bc_rows, grads in sources:
        total = total + jnp.einsum(
            "dj,tj->dt", x_rows, grads[0], preferred_element_type=jnp.float32
        )
        total = total + jnp.einsum(
            "dj,tj->dt", dt_rows, grads[1], preferred_element_type=jnp.float32
        )
        total = total + jnp.einsum(
            "dj,tj->dt", bc_rows.astype(jnp.float32), grads[2], precision=highest
        )
    whole = lax.psum(total, "head")
    grad_share = lax.dynamic_slice_in_dim(whole, lax.axis_index("head") * rows_here, rows_here, 0)
    saliency = jnp.einsum(
        "dt,td->t", whole, layer_in.astype(jnp.float32), precision=highest
    ) / math.sqrt(width)
    return (grad_share, saliency)


def solution(mesh):
    return jax.shard_map(
        shards,
        mesh=mesh,
        in_specs=(
            P("seq"),
            P("seq", None),
            P(),
            P(),
            P(None, "head"),
            P(),
            P(None, "head"),
            P("head"),
            P("head"),
            P("head"),
            P("seq", "head"),
        ),
        out_specs=(P("head", "seq"), P("seq")),
        check_vma=False,
    )
```

profile of v0, /device:TPU:6, one launch (start us, length us, event | category | flops | bytes accessed | tf_op | source)
XLA Modules:
  0.0 731.0 jit_solution(5405587915705148104)
XLA Ops:
  28.8 12.4 %collective-permute-start.30 = (f32[8]{0:T(128)}, f32[8]{0:T(128)}, u32[]{:S(2)}, u32[]{:S(2)}) collective-permute-start(f32[8]{0:T(128)} %fusion.130), channel_id=1, source_target_pairs={{4,0},{8,4},{12,8},{16,12},{20,16},{24,20},{28,24},{32,28},{36,32}... | collective-permute-start | bytes 104 | tf_op jit(solution)/shard_map/ppermute | solution.py:17
  46.9 8.4 %collective-permute-start.37 = (f32[8,64,128]{2,1,0:T(8,128)}, f32[8,64,128]{2,1,0:T(8,128)}, u32[]{:S(2)}, u32[]{:S(2)}) collective-permute-start(f32[8,64,128]{2,1,0:T(8,128)} %fusion.42), channel_id=1, source_target_pairs={{4,0},{8,4},{12,8},{16,12},{20,16},{24,20},{28,24},{32,28},{36,32}... | collective-permute-start | bytes 786440 | tf_op jit(solution)/shard_map/ppermute | solution.py:17
  63.9 9.0 %gather_fusion.3 = bf16[2048,256]{1,0:T(8,128)(2,1)} fusion(bf16[2048,256]{1,0:T(8,128)(2,1)S(1)} %copy-done.1, s32[2048]{0:T(1024)S(1)} %fusion.81), kind=kCustom, calls=%fused_computation.3 | custom fusion | bytes 2105344 | tf_op jit(solution)/shard_map/jit(_take)/gather | solution.py:182
  76.0 9.2 %gather_fusion = bf16[2048,512]{1,0:T(8,128)(2,1)} fusion(bf16[2048,512]{1,0:T(8,128)(2,1)S(1)} %copy-done, s32[2048]{0:T(1024)S(1)} %fusion.81), kind=kCustom, calls=%fused_computation | custom fusion | bytes 4202496 | tf_op jit(solution)/shard_map/jit(_take)/gather | solution.py:180
  87.6 8.8 %gather_fusion.2 = bf16[2048,8]{1,0:T(8,128)(2,1)} fusion(bf16[2048,8]{1,0:T(8,128)(2,1)} %copy.76, s32[2048]{0:T(1024)S(1)} %fusion.81), kind=kCustom, calls=%fused_computation.2 | custom fusion | bytes 73728 | tf_op jit(solution)/shard_map/jit(_take)/gather | solution.py:181
  97.0 8.4 %collective-permute-start.31 = (f32[8]{0:T(128)S(1)}, f32[8]{0:T(128)S(1)}, u32[]{:S(2)}, u32[]{:S(2)}) collective-permute-start(f32[8]{0:T(128)S(1)} %broadcast_select_fusion.5), channel_id=1, source_target_pairs={{4,0},{8,4},{12,8},{16,12},{20,16},{24,20},{28,24},{32,28},{36,32}... | collective-permute-start | bytes 104 | tf_op jit(solution)/shard_map/ppermute | solution.py:17
  137.1 8.8 %collective-permute-start.38 = (f32[8,64,128]{2,1,0:T(8,128)S(1)}, f32[8,64,128]{2,1,0:T(8,128)S(1)}, u32[]{:S(2)}, u32[]{:S(2)}) collective-permute-start(f32[8,64,128]{2,1,0:T(8,128)S(1)} %broadcast_select_fusion.1), channel_id=1, source_target_pairs={{4,0},{8,4},{12,8},{16,12},{20,16},{24,20},{28,24},{32,28},{36,32}... | collective-permute-start | bytes 786440 | tf_op jit(solution)/shard_map/ppermute | solution.py:17
  148.9 15.5 %collective-permute-start.49 = (f32[8]{0:T(128)S(1)}, f32[8]{0:T(128)S(1)}, u32[]{:S(2)}, u32[]{:S(2)}) collective-permute-start(f32[8]{0:T(128)S(1)} %fusion.104), channel_id=1, source_target_pairs={{0,32},{4,36},{8,40},{12,44},{16,48},{20,52},{24,56},{28,60},{32,6... | collective-permute-start | bytes 104 | tf_op jit(solution)/shard_map/ppermute | solution.py:17
  178.3 13.9 %collective-permute-done.39 = f32[8,64,128]{2,1,0:T(8,128)S(1)} collective-permute-done((f32[8,64,128]{2,1,0:T(8,128)S(1)}, f32[8,64,128]{2,1,0:T(8,128)S(1)}, u32[]{:S(2)}, u32[]{:S(2)}) %collective-permute-start.39) | collective-permute-done | bytes 262176 | tf_op jit(solution)/shard_map/ppermute | solution.py:17
  194.2 15.6 %collective-permute-done.54 = f32[8,64,128]{2,1,0:T(8,128)S(1)} collective-permute-done((f32[8,64,128]{2,1,0:T(8,128)S(1)}, f32[8,64,128]{2,1,0:T(8,128)S(1)}, u32[]{:S(2)}, u32[]{:S(2)}) %collective-permute-start.54) | collective-permute-done | bytes 262176 | tf_op jit(solution)/shard_map/ppermute | solution.py:17
  211.9 24.9 %collective-permute-start.50 = (f32[8]{0:T(128)S(1)}, f32[8]{0:T(128)S(1)}, u32[]{:S(2)}, u32[]{:S(2)}) collective-permute-start(f32[8]{0:T(128)S(1)} %fusion.102), channel_id=1, source_target_pairs={{0,64},{4,68},{8,72},{12,76},{16,80},{20,84},{24,88},{28,92},{32,9... | collective-permute-start | bytes 104 | tf_op jit(solution)/shard_map/ppermute | solution.py:17
  244.9 10.1 %collective-permute-start.56 = (f32[8,64,128]{2,1,0:T(8,128)S(1)}, f32[8,64,128]{2,1,0:T(8,128)S(1)}, u32[]{:S(2)}, u32[]{:S(2)}) collective-permute-start(f32[8,64,128]{2,1,0:T(8,128)S(1)} %multiply_add_fusion.4), channel_id=1, source_target_pairs={{0,32},{4,36},{8,40},{12,44},{16,48},{20,52},{24,56},{28,60},{32,6... | collective-permute-start | bytes 786440 | tf_op jit(solution)/shard_map/ppermute | solution.py:17
  266.6 8.7 %collective-permute-start.57 = (f32[8,64,128]{2,1,0:T(8,128)S(1)}, f32[8,64,128]{2,1,0:T(8,128)S(1)}, u32[]{:S(2)}, u32[]{:S(2)}) collective-permute-start(f32[8,64,128]{2,1,0:T(8,128)S(1)} %multiply_add_fusion.3), channel_id=1, source_target_pairs={{0,64},{4,68},{8,72},{12,76},{16,80},{20,84},{24,88},{28,92},{32,9... | collective-permute-start | bytes 786440 | tf_op jit(solution)/shard_map/ppermute | solution.py:17
  334.8 8.4 %collective-permute-start.15 = (f32[8]{0:T(128)}, f32[8]{0:T(128)}, u32[]{:S(2)}, u32[]{:S(2)}) collective-permute-start(f32[8]{0:T(128)} %fusion.129), channel_id=1, source_target_pairs={{4,0},{8,4},{12,8},{16,12},{20,16},{24,20},{28,24},{32,28},{36,32}... | collective-permute-start | bytes 104 | tf_op jit(solution)/shard_map/ppermute | solution.py:17
  357.6 8.4 %collective-permute-start.22 = (f32[8,64,128]{2,1,0:T(8,128)}, f32[8,64,128]{2,1,0:T(8,128)}, u32[]{:S(2)}, u32[]{:S(2)}) collective-permute-start(f32[8,64,128]{2,1,0:T(8,128)} %fusion.52), channel_id=1, source_target_pairs={{4,0},{8,4},{12,8},{16,12},{20,16},{24,20},{28,24},{32,28},{36,32}... | collective-permute-start | bytes 786440 | tf_op jit(solution)/shard_map/ppermute | solution.py:17
  377.4 8.4 %collective-permute-start.16 = (f32[8]{0:T(128)S(1)}, f32[8]{0:T(128)S(1)}, u32[]{:S(2)}, u32[]{:S(2)}) collective-permute-start(f32[8]{0:T(128)S(1)} %broadcast_select_fusion.7), channel_id=1, source_target_pairs={{4,0},{8,4},{12,8},{16,12},{20,16},{24,20},{28,24},{32,28},{36,32}... | collective-permute-start | bytes 104 | tf_op jit(solution)/shard_map/ppermute | solution.py:17
  389.2 8.7 %collective-permute-start.17 = (f32[8]{0:T(128)S(1)}, f32[8]{0:T(128)S(1)}, u32[]{:S(2)}, u32[]{:S(2)}) collective-permute-start(f32[8]{0:T(128)S(1)} %fusion.119), channel_id=1, source_target_pairs={{8,0},{12,4},{16,8},{20,12},{24,16},{28,20},{32,24},{36,28},{40,32... | collective-permute-start | bytes 104 | tf_op jit(solution)/shard_map/ppermute | solution.py:17
  401.9 11.5 %collective-permute-start.18 = (f32[8]{0:T(128)S(1)}, f32[8]{0:T(128)S(1)}, u32[]{:S(2)}, u32[]{:S(2)}) collective-permute-start(f32[8]{0:T(128)S(1)} %fusion.117), channel_id=1, source_target_pairs={{16,0},{20,4},{24,8},{28,12},{32,16},{36,20},{40,24},{44,28},{48,3... | collective-permute-start | bytes 104 | tf_op jit(solution)/shard_map/ppermute | solution.py:17
  413.4 17.3 %collective-permute-start.4 = (f32[8]{0:T(128)S(1)}, f32[8]{0:T(128)S(1)}, u32[]{:S(2)}, u32[]{:S(2)}) collective-permute-start(f32[8]{0:T(128)S(1)} %fusion.103), channel_id=1, source_target_pairs={{0,32},{4,36},{8,40},{12,44},{16,48},{20,52},{24,56},{28,60},{32,6... | collective-permute-start | bytes 104 | tf_op jit(solution)/shard_map/ppermute | solution.py:17
  434.6 8.4 %collective-permute-start.23 = (f32[8,64,128]{2,1,0:T(8,128)S(1)}, f32[8,64,128]{2,1,0:T(8,128)S(1)}, u32[]{:S(2)}, u32[]{:S(2)}) collective-permute-start(f32[8,64,128]{2,1,0:T(8,128)S(1)} %broadcast_select_fusion.2), channel_id=1, source_target_pairs={{4,0},{8,4},{12,8},{16,12},{20,16},{24,20},{28,24},{32,28},{36,32}... | collective-permute-start | bytes 786440 | tf_op jit(solution)/shard_map/ppermute | solution.py:17
  470.6 8.8 %collective-permute-start.25 = (f32[8,64,128]{2,1,0:T(8,128)S(1)}, f32[8,64,128]{2,1,0:T(8,128)S(1)}, u32[]{:S(2)}, u32[]{:S(2)}) collective-permute-start(f32[8,64,128]{2,1,0:T(8,128)S(1)} %multiply_add_fusion.19), channel_id=1, source_target_pairs={{16,0},{20,4},{24,8},{28,12},{32,16},{36,20},{40,24},{44,28},{48,3... | collective-permute-start | bytes 786440 | tf_op jit(solution)/shard_map/ppermute | solution.py:17
  481.4 25.2 %collective-permute-done.10 = f32[8,64,128]{2,1,0:T(8,128)S(1)} collective-permute-done((f32[8,64,128]{2,1,0:T(8,128)S(1)}, f32[8,64,128]{2,1,0:T(8,128)S(1)}, u32[]{:S(2)}, u32[]{:S(2)}) %collective-permute-start.10) | collective-permute-done | bytes 262176 | tf_op jit(solution)/shard_map/ppermute | solution.py:17
  523.2 11.9 %collective-permute-start.12 = (f32[8,64,128]{2,1,0:T(8,128)S(1)}, f32[8,64,128]{2,1,0:T(8,128)S(1)}, u32[]{:S(2)}, u32[]{:S(2)}) collective-permute-start(f32[8,64,128]{2,1,0:T(8,128)S(1)} %multiply_add_fusion.24), channel_id=1, source_target_pairs={{0,64},{4,68},{8,72},{12,76},{16,80},{20,84},{24,88},{28,92},{32,9... | collective-permute-start | bytes 786440 | tf_op jit(solution)/shard_map/ppermute | solution.py:17
  606.3 114.1 %all-reduce.4.cloned.1.call-done = f32[2048,128]{0,1:T(8,128)} async-done(((f32[2048,128]{0,1:T(8,128)}), f32[2048,128]{0,1:T(8,128)}) %all-reduce.4.cloned.1.call-update) | async-done | bytes 1048592 | tf_op jit(solution)/shard_map/psum | solution.py:197
  (354 shorter events, 330.2 us)
Async XLA Ops:
  7.2 713.3 %all-reduce.4.cloned.1.call-start = ((), (), s32[]{:S(2)}) async-start(), calls=%async_computation | async-start | bytes 2097152 | tf_op jit(solution)/shard_map/psum | solution.py:197
  28.8 67.5 %collective-permute-start.30 = (f32[8]{0:T(128)}, f32[8]{0:T(128)}, u32[]{:S(2)}, u32[]{:S(2)}) collective-permute-start(f32[8]{0:T(128)} %fusion.130), channel_id=1, source_target_pairs={{4,0},{8,4},{12,8},{16,12},{20,16},{24,20},{28,24},{32,28},{36,32}... | collective-permute-start | bytes 104 | tf_op jit(solution)/shard_map/ppermute | solution.py:17
  41.3 64.1 %collective-permute-start.45 = (f32[8]{0:T(128)}, f32[8]{0:T(128)}, u32[]{:S(2)}, u32[]{:S(2)}) collective-permute-start(f32[8]{0:T(128)} %fusion.130), channel_id=1, source_target_pairs={{0,4},{4,8},{8,12},{12,16},{16,20},{20,24},{24,28},{28,32},{32,36}... | collective-permute-start | bytes 104 | tf_op jit(solution)/shard_map/ppermute | solution.py:17
  46.9 89.2 %collective-permute-start.37 = (f32[8,64,128]{2,1,0:T(8,128)}, f32[8,64,128]{2,1,0:T(8,128)}, u32[]{:S(2)}, u32[]{:S(2)}) collective-permute-start(f32[8,64,128]{2,1,0:T(8,128)} %fusion.42), channel_id=1, source_target_pairs={{4,0},{8,4},{12,8},{16,12},{20,16},{24,20},{28,24},{32,28},{36,32}... | collective-permute-start | bytes 786440 | tf_op jit(solution)/shard_map/ppermute | solution.py:17
  60.8 85.2 %collective-permute-start.52 = (f32[8,64,128]{2,1,0:T(8,128)}, f32[8,64,128]{2,1,0:T(8,128)}, u32[]{:S(2)}, u32[]{:S(2)}) collective-permute-start(f32[8,64,128]{2,1,0:T(8,128)} %fusion.40), channel_id=1, source_target_pairs={{0,4},{4,8},{8,12},{12,16},{16,20},{20,24},{24,28},{28,32},{32,36}... | collective-permute-start | bytes 786440 | tf_op jit(solution)/shard_map/ppermute | solution.py:17
  133.7 42.7 %collective-permute-start.34 = (f32[8]{0:T(128)S(1)}, f32[8]{0:T(128)S(1)}, u32[]{:S(2)}, u32[]{:S(2)}) collective-permute-start(f32[8]{0:T(128)S(1)} %fusion.116), channel_id=1, source_target_pairs={{32,0},{36,4},{40,8},{44,12},{48,16},{52,20},{56,24},{60,28},{64,3... | collective-permute-start | bytes 104 | tf_op jit(solution)/shard_map/ppermute | solution.py:17
  148.9 62.9 %collective-permute-start.49 = (f32[8]{0:T(128)S(1)}, f32[8]{0:T(128)S(1)}, u32[]{:S(2)}, u32[]{:S(2)}) collective-permute-start(f32[8]{0:T(128)S(1)} %fusion.104), channel_id=1, source_target_pairs={{0,32},{4,36},{8,40},{12,44},{16,48},{20,52},{24,56},{28,60},{32,6... | collective-permute-start | bytes 104 | tf_op jit(solution)/shard_map/ppermute | solution.py:17
  168.5 41.3 %collective-permute-start.54 = (f32[8,64,128]{2,1,0:T(8,128)S(1)}, f32[8,64,128]{2,1,0:T(8,128)S(1)}, u32[]{:S(2)}, u32[]{:S(2)}) collective-permute-start(f32[8,64,128]{2,1,0:T(8,128)S(1)} %multiply_add_fusion.6), channel_id=1, source_target_pairs={{0,8},{4,12},{8,16},{12,20},{16,24},{20,28},{24,32},{28,36},{32,40... | collective-permute-start | bytes 786440 | tf_op jit(solution)/shard_map/ppermute | solution.py:17
  176.4 78.7 %collective-permute-start.35 = (f32[8]{0:T(128)S(1)}, f32[8]{0:T(128)S(1)}, u32[]{:S(2)}, u32[]{:S(2)}) collective-permute-start(f32[8]{0:T(128)S(1)} %fusion.114), channel_id=1, source_target_pairs={{64,0},{68,4},{72,8},{76,12},{80,16},{84,20},{88,24},{92,28},{96,3... | collective-permute-start | bytes 104 | tf_op jit(solution)/shard_map/ppermute | solution.py:17
  192.3 45.3 %collective-permute-start.40 = (f32[8,64,128]{2,1,0:T(8,128)S(1)}, f32[8,64,128]{2,1,0:T(8,128)S(1)}, u32[]{:S(2)}, u32[]{:S(2)}) collective-permute-start(f32[8,64,128]{2,1,0:T(8,128)S(1)} %multiply_add_fusion.12), channel_id=1, source_target_pairs={{16,0},{20,4},{24,8},{28,12},{32,16},{36,20},{40,24},{44,28},{48,3... | collective-permute-start | bytes 786440 | tf_op jit(solution)/shard_map/ppermute | solution.py:17
  209.9 34.9 %collective-permute-start.55 = (f32[8,64,128]{2,1,0:T(8,128)S(1)}, f32[8,64,128]{2,1,0:T(8,128)S(1)}, u32[]{:S(2)}, u32[]{:S(2)}) collective-permute-start(f32[8,64,128]{2,1,0:T(8,128)S(1)} %multiply_add_fusion.5), channel_id=1, source_target_pairs={{0,16},{4,20},{8,24},{12,28},{16,32},{20,36},{24,40},{28,44},{32,4... | collective-permute-start | bytes 786440 | tf_op jit(solution)/shard_map/ppermute | solution.py:17
  211.9 63.4 %collective-permute-start.50 = (f32[8]{0:T(128)S(1)}, f32[8]{0:T(128)S(1)}, u32[]{:S(2)}, u32[]{:S(2)}) collective-permute-start(f32[8]{0:T(128)S(1)} %fusion.102), channel_id=1, source_target_pairs={{0,64},{4,68},{8,72},{12,76},{16,80},{20,84},{24,88},{28,92},{32,9... | collective-permute-start | bytes 104 | tf_op jit(solution)/shard_map/ppermute | solution.py:17
  332.8 41.3 %collective-permute-start = (f32[8]{0:T(128)}, f32[8]{0:T(128)}, u32[]{:S(2)}, u32[]{:S(2)}) collective-permute-start(f32[8]{0:T(128)} %fusion.129), channel_id=1, source_target_pairs={{0,4},{4,8},{8,12},{12,16},{16,20},{20,24},{24,28},{28,32},{32,36}... | collective-permute-start | bytes 104 | tf_op jit(solution)/shard_map/ppermute | solution.py:17
  334.8 42.0 %collective-permute-start.15 = (f32[8]{0:T(128)}, f32[8]{0:T(128)}, u32[]{:S(2)}, u32[]{:S(2)}) collective-permute-start(f32[8]{0:T(128)} %fusion.129), channel_id=1, source_target_pairs={{4,0},{8,4},{12,8},{16,12},{20,16},{24,20},{28,24},{32,28},{36,32}... | collective-permute-start | bytes 104 | tf_op jit(solution)/shard_map/ppermute | solution.py:17
  353.7 77.0 %collective-permute-start.7 = (f32[8,64,128]{2,1,0:T(8,128)}, f32[8,64,128]{2,1,0:T(8,128)}, u32[]{:S(2)}, u32[]{:S(2)}) collective-permute-start(f32[8,64,128]{2,1,0:T(8,128)} %fusion.54), channel_id=1, source_target_pairs={{0,4},{4,8},{8,12},{12,16},{16,20},{20,24},{24,28},{28,32},{32,36}... | collective-permute-start | bytes 786440 | tf_op jit(solution)/shard_map/ppermute | solution.py:17
  357.6 76.1 %collective-permute-start.22 = (f32[8,64,128]{2,1,0:T(8,128)}, f32[8,64,128]{2,1,0:T(8,128)}, u32[]{:S(2)}, u32[]{:S(2)}) collective-permute-start(f32[8,64,128]{2,1,0:T(8,128)} %fusion.52), channel_id=1, source_target_pairs={{4,0},{8,4},{12,8},{16,12},{20,16},{24,20},{28,24},{32,28},{36,32}... | collective-permute-start | bytes 786440 | tf_op jit(solution)/shard_map/ppermute | solution.py:17
  401.9 41.2 %collective-permute-start.18 = (f32[8]{0:T(128)S(1)}, f32[8]{0:T(128)S(1)}, u32[]{:S(2)}, u32[]{:S(2)}) collective-permute-start(f32[8]{0:T(128)S(1)} %fusion.117), channel_id=1, source_target_pairs={{16,0},{20,4},{24,8},{28,12},{32,16},{36,20},{40,24},{44,28},{48,3... | collective-permute-start | bytes 104 | tf_op jit(solution)/shard_map/ppermute | solution.py:17
  413.4 44.4 %collective-permute-start.4 = (f32[8]{0:T(128)S(1)}, f32[8]{0:T(128)S(1)}, u32[]{:S(2)}, u32[]{:S(2)}) collective-permute-start(f32[8]{0:T(128)S(1)} %fusion.103), channel_id=1, source_target_pairs={{0,32},{4,36},{8,40},{12,44},{16,48},{20,52},{24,56},{28,60},{32,6... | collective-permute-start | bytes 104 | tf_op jit(solution)/shard_map/ppermute | solution.py:17
  443.1 36.3 %collective-permute-start.19 = (f32[8]{0:T(128)S(1)}, f32[8]{0:T(128)S(1)}, u32[]{:S(2)}, u32[]{:S(2)}) collective-permute-start(f32[8]{0:T(128)S(1)} %fusion.115), channel_id=1, source_target_pairs={{32,0},{36,4},{40,8},{44,12},{48,16},{52,20},{56,24},{60,28},{64,3... | collective-permute-start | bytes 104 | tf_op jit(solution)/shard_map/ppermute | solution.py:17
  457.9 61.8 %collective-permute-start.5 = (f32[8]{0:T(128)S(1)}, f32[8]{0:T(128)S(1)}, u32[]{:S(2)}, u32[]{:S(2)}) collective-permute-start(f32[8]{0:T(128)S(1)} %fusion.101), channel_id=1, source_target_pairs={{0,64},{4,68},{8,72},{12,76},{16,80},{20,84},{24,88},{28,92},{32,9... | collective-permute-start | bytes 104 | tf_op jit(solution)/shard_map/ppermute | solution.py:17
  463.8 42.7 %collective-permute-start.10 = (f32[8,64,128]{2,1,0:T(8,128)S(1)}, f32[8,64,128]{2,1,0:T(8,128)S(1)}, u32[]{:S(2)}, u32[]{:S(2)}) collective-permute-start(f32[8,64,128]{2,1,0:T(8,128)S(1)} %multiply_add_fusion.26), channel_id=1, source_target_pairs={{0,16},{4,20},{8,24},{12,28},{16,32},{20,36},{24,40},{28,44},{32,4... | collective-permute-start | bytes 786440 | tf_op jit(solution)/shard_map/ppermute | solution.py:17
  470.6 47.1 %collective-permute-start.25 = (f32[8,64,128]{2,1,0:T(8,128)S(1)}, f32[8,64,128]{2,1,0:T(8,128)S(1)}, u32[]{:S(2)}, u32[]{:S(2)}) collective-permute-start(f32[8,64,128]{2,1,0:T(8,128)S(1)} %multiply_add_fusion.19), channel_id=1, source_target_pairs={{16,0},{20,4},{24,8},{28,12},{32,16},{36,20},{40,24},{44,28},{48,3... | collective-permute-start | bytes 786440 | tf_op jit(solution)/shard_map/ppermute | solution.py:17
  479.4 57.7 %collective-permute-start.20 = (f32[8]{0:T(128)S(1)}, f32[8]{0:T(128)S(1)}, u32[]{:S(2)}, u32[]{:S(2)}) collective-permute-start(f32[8]{0:T(128)S(1)} %fusion.113), channel_id=1, source_target_pairs={{64,0},{68,4},{72,8},{76,12},{80,16},{84,20},{88,24},{92,28},{96,3... | collective-permute-start | bytes 104 | tf_op jit(solution)/shard_map/ppermute | solution.py:17
  519.7 33.3 %collective-permute-start.6 = (f32[8]{0:T(128)S(1)}, f32[8]{0:T(128)S(1)}, u32[]{:S(2)}, u32[]{:S(2)}) collective-permute-start(f32[8]{0:T(128)S(1)} %fusion.99), channel_id=1, source_target_pairs={{0,128},{4,132},{8,136},{12,140},{16,144},{20,148},{24,152},{28,15... | collective-permute-start | bytes 104 | tf_op jit(solution)/shard_map/ppermute | solution.py:17
  (84 other events, 1129.2 us)
Sparse Core Ops, SparseCore 0:
  606.5 113.9 all-reduce.3
where the time goes:
time: 735 us; the launch traced here: 731 us
  starting transfers between devices  321 us (44%)
  waiting for transfers between devices  222 us (30%)
  local copies, waits for them, and re-layouts  74 us (10%)
  matrix products  55.2 us (8%)
  other arithmetic  43 us (6%)
  between operations  15.7 us (2%)
    ppermute x60, starting transfers between devices, shifted(): lax.ppermute(value, axis, [(source, source + steps) for source in range(f...  321 us
    psum x1, waiting for transfers between devices, shards(): whole = lax.psum(total, 'head')  114 us
    ppermute x60, waiting for transfers between devices, shifted(): lax.ppermute(value, axis, [(source, source + steps) for source in range(f...  108 us
  transfers between devices with their start and end apart: 61, of which 22 were waited for; matrix products, arithmetic and copies ran while one was open for 11% of the time, Pallas kernels for 0%

commit v1 on v0

v1 whole, which is shorter than its diff:
```python
import functools
import math

import jax
import jax.numpy as jnp
from jax import lax
from jax.experimental import pallas as pl
from jax.experimental.pallas import tpu as pltpu
from jax.sharding import PartitionSpec as P

L = 128
H = 8
HP = 512
N = 128
WIDTH = 2048
TILE = 256
F32 = jnp.float32
BF16 = jnp.bfloat16
NEG = -1e30
MESH = pl.DeviceIdType.MESH

NN = (((1,), (0,)), ((), ()))
NT = (((1,), (1,)), ((), ()))
TN = (((0,), (0,)), ((), ()))


def exact(a, b, dims=NN):
    return lax.dot_general(a, b, dims, precision=lax.Precision.HIGHEST, preferred_element_type=F32)


def fast(a, b, dims=NN):
    return lax.dot_general(a.astype(BF16), b.astype(BF16), dims, preferred_element_type=F32)


def iota(shape, axis):
    return lax.broadcasted_iota(jnp.int32, shape, axis)


def head_rows():
    return (iota((H, HP), 1) // 64 == iota((H, HP), 0)).astype(F32)


def reach(branch):
    row, col = iota((L, L), 0), iota((L, L), 1)
    return col <= row if branch == 0 else col >= row


def rates(pre, bias, rate):
    z = pre + bias
    stride = jnp.maximum(z, 0.0) + jnp.log1p(jnp.exp(-jnp.abs(z)))
    return z, stride, -rate * stride


def embed(tokens_row, embedding, residual):
    vocab = embedding.shape[0]
    hot = (iota((vocab, L), 0) == tokens_row).astype(F32).T.astype(BF16)
    return (
        jnp.dot(hot, embedding, preferred_element_type=F32) + residual.astype(F32)
    ).astype(BF16)


def summaries(branch, x, mixed, pre, bias, rate, upstream):
    _, stride, log_decay = rates(pre, bias, rate)
    run = exact(reach(branch).astype(F32), log_decay)
    total = jnp.sum(log_decay, axis=0, keepdims=True)
    spread = head_rows()
    carry = exact(jnp.exp(total - run) * stride, spread)
    grown = exact(jnp.exp(run), spread)
    end = fast((x * carry).T, mixed[:, :N])
    direct = fast((upstream * grown).T, mixed[:, N:])
    return jnp.exp(total), end, direct


def backward(branch, x, mixed, pre, bias, rate, skip, upstream, entry, later):
    writer, reader = mixed[:, :N], mixed[:, N:]
    z, stride, log_decay = rates(pre, bias, rate)
    mask = reach(branch)
    mask_t = reach(1 - branch)
    run = exact(mask.astype(F32), log_decay)
    run_t = run.T
    total = jnp.sum(log_decay, axis=0, keepdims=True)
    spread = head_rows()
    stride_e = exact(stride, spread)
    decay_e = exact(jnp.exp(total - run), spread)
    grown = upstream * exact(jnp.exp(run), spread)
    carried = x * stride_e * decay_e
    low_half = iota((L, 2 * 64), 1) < 64
    scores_t = fast(writer, reader, NT)
    ups = upstream.astype(F32)
    volume = jnp.zeros((L, L), F32)
    rows = []
    pieces = []
    for pair in range(H // 2):
        lanes = slice(128 * pair, 128 * pair + 128)
        x_pair, u_pair = x[:, lanes], ups[:, lanes]
        kernels, uppers = [], []
        for half in range(2):
            h = 2 * pair + half
            mine = low_half if half == 0 else jnp.logical_not(low_half)
            u_half = jnp.where(mine, u_pair, 0.0)
            fade = jnp.exp(jnp.where(mask_t, run_t[h : h + 1, :] - run[:, h : h + 1], NEG))
            cross = fast(x_pair, u_half, NT)
            weight = fade * cross * stride[:, h : h + 1]
            volume = volume + weight
            rows.append(jnp.sum(weight * scores_t, axis=0, keepdims=True))
            kernels.append((fade * scores_t).astype(BF16))
            uppers.append(u_half.astype(BF16))
        pieces.append(fast(jnp.concatenate(kernels, axis=1), jnp.concatenate(uppers, axis=0)))
    pushed = fast(writer, later, NT)
    inner = jnp.concatenate(pieces, axis=1) + decay_e * pushed
    d_inputs = exact(skip, spread) * ups + stride_e * inner
    d_writer = fast(volume, reader) + fast(carried, later)
    d_reader = fast(volume.T, writer) + fast(grown, entry)
    pulled = fast(reader, entry, NT)
    spread_t = spread.T
    per_write = exact(x * inner, spread_t)
    tail = exact(carried * pushed, spread_t)
    per_read = jnp.concatenate(rows, axis=0).T + exact(grown * pulled, spread_t)
    dots = exact(spread, entry * later)
    overlap = exact(jnp.ones((8, L), F32), dots, NT)[0:1]
    d_total = jnp.exp(total) * overlap + jnp.sum(tail, axis=0, keepdims=True)
    d_run = per_read - stride * per_write
    d_log = exact(mask_t.astype(F32), d_run) + d_total
    d_stride = per_write - rate * d_log
    d_pre = d_stride / (1.0 + jnp.exp(-z))
    return d_inputs, d_pre, d_writer, d_reader


def project(source, x_weight, bc_weight, dt_weight):
    dot = functools.partial(jnp.dot, preferred_element_type=F32)
    return dot(source, x_weight), dot(source, bc_weight), dot(source, dt_weight)


def permutation(pairing_row, first, count, axis):
    shape = (WIDTH, count) if axis == 1 else (count, WIDTH)
    return (iota(shape, 0) + (0 if axis == 1 else first) == pairing_row).astype(F32).astype(BF16)


def padded_rows(factor, first):
    wide = jnp.broadcast_to(factor, (H, H))
    own = jnp.where(iota((H, H), 0) + first == iota((H, H), 1), wide, 0.0)
    return jnp.broadcast_to(jnp.sum(own, axis=1, keepdims=True), (H, N))


def front_kernel(
    tokens, residual, pairing, embedding, x_weight, bc_weight, dt_weight, bias, rate, cotangent,
    x_out, mixed_out, pre_out, layer_t, sums, source,
):
    layer = embed(tokens[...], embedding[...], residual[...])
    layer_t[...] = layer.astype(F32).T.astype(BF16)
    for block in range(WIDTH // TILE):
        cols = slice(TILE * block, TILE * block + TILE)
        hot = permutation(pairing[:, cols], 0, TILE, 1)
        source[:, cols] = jnp.dot(layer, hot, preferred_element_type=F32).astype(BF16)
    upstream = cotangent[...].astype(F32)
    for branch in range(2):
        read = layer if branch == 0 else source[...]
        x, mixed, pre = project(read, x_weight[...], bc_weight[...], dt_weight[...])
        x_out[branch] = x
        mixed_out[branch] = mixed
        pre_out[branch] = pre
        factor, end, direct = summaries(branch, x, mixed, pre, bias[...], rate[...], upstream)
        up, down = (end, direct) if branch == 0 else (direct, end)
        for way, value in ((0, up), (1, down)):
            for part in range(2):
                piece = 2 * branch + part
                sums[way, piece, 0:256, :] = value[256 * part : 256 * part + 256]
                sums[way, piece, 256:264, :] = padded_rows(factor, 4 * part)


def scaled(factors, values):
    return jnp.concatenate(
        [factors[i : i + 1, :] * values[64 * i : 64 * i + 64, :] for i in range(4)], axis=0
    )


def after(later, earlier):
    values = scaled(later[256:264], earlier[0:256]) + later[0:256]
    return jnp.concatenate([values, later[256:264] * earlier[256:264]], axis=0)


def scan_kernel(sums, out, partner, chip, z_in, z_pre, x_in, y_in, e_line, e_out, e_in, far, far_in, send, recv):
    seq, head = lax.axis_index("seq"), lax.axis_index("head")
    core = lax.rem(seq, 2)
    z = lax.rem(seq // 2, 4)
    x = lax.rem(seq // 8, 4)
    y = seq // 32

    def device(yy, xx, zz, cc):
        return (((yy * 4 + xx) * 4 + zz) * 2 + cc, head)

    def other(value, step):
        return lax.rem(value + step, 4)

    mate = device(y, x, z, 1 - core)
    z_peer = [device(y, x, other(z, d), core) for d in (1, 2, 3)]
    x_peer = [device(y, other(x, d), z, core) for d in (1, 2, 3)]
    y_peer = [device(other(y, d), x, z, core) for d in (1, 2, 3)]
    barrier = pltpu.get_barrier_semaphore()
    for peer in [mate] + z_peer + x_peer + y_peer:
        pl.semaphore_signal(barrier, inc=1, device_id=peer, device_id_type=MESH)
    pl.semaphore_wait(barrier, 10)

    def push(source, target, slot, peer):
        copy = pltpu.make_async_remote_copy(
            src_ref=source, dst_ref=target, send_sem=send.at[slot], recv_sem=recv.at[slot],
            device_id=peer, device_id_type=MESH,
        )
        copy.start()
        return copy

    first = [push(sums.at[1 - core, q], partner.at[q], q, mate) for q in range(4)]
    for q in range(4):
        first[q].wait_recv()
        chip[q] = after(partner[q], sums[core, q])
    z_copies = [push(chip.at[other(z, d)], z_in.at[z], 3 + d, z_peer[d - 1]) for d in (1, 2, 3)]
    z_in[z] = chip[z]
    for copy in z_copies:
        copy.wait_recv()

    def place(j):
        return jnp.where(core == 0, j, 3 - j)

    line = z_in[place(0)]
    for j in range(1, 4):
        z_pre[place(j)] = line
        line = after(z_in[place(j)], line)
    x_in[x] = line
    x_copies = [push(x_in.at[x], x_in.at[x], 6 + d, x_peer[d - 1]) for d in (1, 2, 3)]
    for copy in x_copies:
        copy.wait_recv()
    blank = jnp.concatenate([jnp.zeros((256, N), F32), jnp.ones((8, N), F32)], axis=0)

    def before(held, mine):
        total, prefix = blank, blank
        for j in range(4):
            spot = place(j)
            prefix = jnp.where(spot == mine, total, prefix)
            total = after(held[spot], total)
        return prefix, total

    x_prefix, x_total = before(x_in, x)
    y_in[y] = x_total
    y_copies = [push(y_in.at[y], y_in.at[y], 9 + d, y_peer[d - 1]) for d in (1, 2, 3)]
    for copy in y_copies:
        copy.wait_recv()
    y_prefix, _ = before(y_in, y)
    e_line[...] = after(x_prefix, y_prefix)
    e_out[place(0)] = e_line[0:256, :]
    for j in range(1, 4):
        held = z_pre[place(j)]
        e_out[place(j)] = scaled(held[256:264], e_line[0:256, :]) + held[0:256]
    e_copies = [push(e_out.at[other(z, d)], e_in.at[z], 12 + d, z_peer[d - 1]) for d in (1, 2, 3)]
    e_in[z] = e_out[z]
    for copy in e_copies:
        copy.wait_recv()
    for q in range(4):
        value = sums[core, q]
        far[q] = scaled(value[256:264], e_in[q]) + value[0:256]
        out[core, q] = e_in[q]
    last = [push(far.at[q], far_in.at[q], 16 + q, mate) for q in range(4)]
    for q in range(4):
        last[q].wait_recv()
        out[1 - core, q] = far_in[q]
    for copy in first + z_copies + x_copies + y_copies + e_copies + last:
        copy.wait_send()


def grad_kernel(x, mixed, pre, bias, rate, skip, cotangent, states, d_x, d_mixed, d_pre):
    upstream = cotangent[...].astype(F32)
    for branch in range(2):
        way = (0, 1) if branch == 0 else (1, 0)

        def whole(direction):
            return jnp.concatenate([states[direction, 2 * branch], states[direction, 2 * branch + 1]], axis=0)

        entry, later = whole(way[0]), whole(way[1])
        g_x, g_pre, g_writer, g_reader = backward(
            branch, x[branch], mixed[branch], pre[branch], bias[...], rate[...], skip[...],
            upstream, entry, later,
        )
        d_x[branch] = g_x.astype(BF16)
        d_pre[branch] = g_pre.astype(BF16)
        for column, value in ((0, g_writer), (N, g_reader)):
            high = value.astype(BF16)
            d_mixed[branch, 0, :, column : column + N] = high
            d_mixed[branch, 1, :, column : column + N] = (value - high.astype(F32)).astype(BF16)


def paired_kernel(pairing, x_weight, bc_weight, dt_weight, x_out, bc_out, dt_out):
    for block in range(WIDTH // TILE):
        rows = slice(TILE * block, TILE * block + TILE)
        hot = permutation(pairing[...], TILE * block, TILE, 0)
        for weight, target in ((x_weight, x_out), (bc_weight, bc_out), (dt_weight, dt_out)):
            target[rows, :] = jnp.dot(hot, weight[...], preferred_element_type=F32).astype(BF16)


def back_kernel(
    x_weight, bc_weight, dt_weight, x_paired, bc_paired, dt_paired, d_x, d_mixed, d_pre, layer_t,
    grad, saliency, part, got, sal_part, sal_got, send, recv,
):
    seq, head = lax.axis_index("seq"), lax.axis_index("head")

    def peer(step):
        return (seq, lax.rem(head + step, 4))

    barrier = pltpu.get_barrier_semaphore()
    for step in (1, 2, 3):
        pl.semaphore_signal(barrier, inc=1, device_id=peer(step), device_id_type=MESH)
    pl.semaphore_wait(barrier, 3)
    rows_here = WIDTH // 4

    def push(source, target, slot, device):
        copy = pltpu.make_async_remote_copy(
            src_ref=source, dst_ref=target, send_sem=send.at[slot], recv_sem=recv.at[slot],
            device_id=device, device_id_type=MESH,
        )
        copy.start()
        return copy

    def chunk(owner):
        rows = pl.ds(pl.multiple_of(owner * rows_here, rows_here), rows_here)
        total = jnp.zeros((rows_here, L), F32)
        for branch, weights in (
            (0, (x_weight, bc_weight, dt_weight)),
            (1, (x_paired, bc_paired, dt_paired)),
        ):
            total = total + lax.dot_general(weights[0][rows, :], d_x[branch], NT, preferred_element_type=F32)
            for term in range(2):
                total = total + lax.dot_general(
                    weights[1][rows, :], d_mixed[branch, term], NT, preferred_element_type=F32
                )
            total = total + lax.dot_general(weights[2][rows, :], d_pre[branch], NT, preferred_element_type=F32)
        weighed = jnp.sum(total * layer_t[rows, :].astype(F32), axis=0, keepdims=True)
        return total, weighed

    copies = []
    weighed = jnp.zeros((1, L), F32)
    for step in (1, 2, 3):
        owner = lax.rem(head + step, 4)
        total, share = chunk(owner)
        weighed = weighed + share
        part[step - 1] = total
        copies.append(push(part.at[step - 1], got.at[step - 1], step - 1, peer(step)))
    total, share = chunk(head)
    weighed = weighed + share
    sal_part[...] = jnp.broadcast_to(weighed, (8, L))
    sal_got[head] = sal_part[...]
    for step in (1, 2, 3):
        copies.append(push(sal_part, sal_got.at[head], 2 + step, peer(step)))
    for copy in copies:
        copy.wait_recv()
    grad[...] = ((total + got[0]) + got[1]) + got[2]
    saliency[...] = (
        ((sal_got[0, 0:1] + sal_got[1, 0:1]) + sal_got[2, 0:1]) + sal_got[3, 0:1]
    ) / math.sqrt(WIDTH)
    for copy in copies:
        copy.wait_send()


VM = pl.BlockSpec(memory_space=pltpu.VMEM)


def call(kernel, outs, count, scratch=(), comm=None):
    return pl.pallas_call(
        kernel,
        out_shape=[jax.ShapeDtypeStruct(shape, dtype) for shape, dtype in outs],
        in_specs=[VM] * count,
        out_specs=[VM] * len(outs),
        scratch_shapes=list(scratch),
        compiler_params=pltpu.CompilerParams(
            collective_id=comm, has_side_effects=comm is not None, vmem_limit_bytes=60 << 20
        ),
    )


def shards(
    tokens, residual_in, pairing, embedding, x_weight, bc_weight, dt_weight, dt_bias, decay_rate,
    skip_gain, cotangent,
):
    tokens_row, pairing_row = tokens.reshape(1, L), pairing.reshape(1, WIDTH)
    bias, rate, skip = (value.reshape(1, H) for value in (dt_bias, decay_rate, skip_gain))
    x, mixed, pre, layer_t, sums = call(
        front_kernel,
        [
            ((2, L, HP), F32), ((2, L, 2 * N), F32), ((2, L, H), F32), ((WIDTH, L), BF16),
            ((2, 4, 264, N), F32),
        ],
        10,
        [pltpu.VMEM((L, WIDTH), BF16)],
    )(tokens_row, residual_in, pairing_row, embedding, x_weight, bc_weight, dt_weight, bias, rate, cotangent)
    block = pltpu.VMEM((4, 264, N), F32)
    plain = pltpu.VMEM((4, 256, N), F32)
    (states,) = call(
        scan_kernel,
        [((2, 4, 256, N), F32)],
        1,
        [
            block, block, block, block, block, block, pltpu.VMEM((264, N), F32), plain, plain,
            plain, plain, pltpu.SemaphoreType.DMA((20,)), pltpu.SemaphoreType.DMA((20,)),
        ],
        comm=0,
    )(sums)
    x_paired, bc_paired, dt_paired = call(
        paired_kernel, [((WIDTH, HP), BF16), ((WIDTH, 2 * N), BF16), ((WIDTH, H), BF16)], 4
    )(pairing_row, x_weight, bc_weight, dt_weight)
    d_x, d_mixed, d_pre = call(
        grad_kernel,
        [((2, L, HP), BF16), ((2, 2, L, 2 * N), BF16), ((2, L, H), BF16)],
        8,
    )(x, mixed, pre, bias, rate, skip, cotangent, states)
    grad, saliency = call(
        back_kernel,
        [((WIDTH // 4, L), F32), ((1, L), F32)],
        10,
        [
            pltpu.VMEM((3, WIDTH // 4, L), F32), pltpu.VMEM((3, WIDTH // 4, L), F32),
            pltpu.VMEM((8, L), F32), pltpu.VMEM((4, 8, L), F32),
            pltpu.SemaphoreType.DMA((6,)), pltpu.SemaphoreType.DMA((6,)),
        ],
        comm=1,
    )(x_weight, bc_weight, dt_weight, x_paired, bc_paired, dt_paired, d_x, d_mixed, d_pre, layer_t)
    return grad, saliency.reshape(L)


def solution(mesh):
    return jax.shard_map(
        shards,
        mesh=mesh,
        in_specs=(
            P("seq"), P("seq", None), P(), P(), P(None, "head"), P(), P(None, "head"), P("head"),
            P("head"), P("head"), P("seq", "head"),
        ),
        out_specs=(P("head", "seq"), P("seq")),
        check_vma=False,
    )
```

time: 735 us -> 158 us (0.21)
  starting transfers between devices: 321 us -> 0 us
  waiting for transfers between devices: 222 us -> 0 us
  Pallas kernels: 0 us -> 152 us
  local copies, waits for them, and re-layouts: 74 us -> 4.61 us
  matrix products: 55.2 us -> 0 us
  other arithmetic: 43 us -> 0 us
  between operations: 15.7 us -> 0.65 us
    ppermute x60 -> x0, starting transfers between devices: 321 us -> none  [shifted(): lax.ppermute(value, axis, [(source, source + steps) for source in range(f...]
    pallas_call x0 -> x5, Pallas kernels: none -> 152 us  [the longest x1 91.5 us: shards(): call(scan_kernel, [((2, 4, 256, N), F32)], 1, [block, block, block, block...]
    psum x1 -> x0, waiting for transfers between devices: 114 us -> none  [shards(): whole = lax.psum(total, 'head')]
    ppermute x60 -> x0, waiting for transfers between devices: 108 us -> none  [shifted(): lax.ppermute(value, axis, [(source, source + steps) for source in range(f...]
    dot_general x35 -> x0, matrix products: 55.2 us -> none  [the longest x4 9.24 us: advance(): within = jnp.einsum('qsh,shp->qhp', weights, in_block, precision=highest)]
    gather x4 -> x0, local copies, waits for them, and re-layouts: 34.9 us -> none  [the longest x1 9.15 us: shards(): jnp.take(x_weight, pairing, axis=0)]
    rev x5 -> x0, local copies, waits for them, and re-layouts: 10.7 us -> none  [the longest x1 5.59 us: shards(): reverse_proj = project(jnp.flip(paired, 0))]
    add x28 -> x0, other arithmetic: 9.19 us -> none  [combine(): joined.append(later[0][:, None, None] * earlier[1] + later[1])]
  transfers between devices with their start and end apart: 61 -> 0, of which waited for: 22 -> 0; matrix products, arithmetic and copies ran while one was open for 11% -> 0% of each run, Pallas kernels for 0% -> 0%
where the time goes in v1:
time: 158 us; the launch traced here: 157 us
  Pallas kernels  152 us (96%)
  local copies, waits for them, and re-layouts  4.61 us (3%)
    pallas_call x1, Pallas kernels, shards(): call(scan_kernel, [((2, 4, 256, N), F32)], 1, [block, block, block, block...  91.5 us
    pallas_call x1, Pallas kernels, shards(): call(back_kernel, [((WIDTH // 4, L), F32), ((1, L), F32)], 10, [pltpu.VME...  33.2 us
    pallas_call x1, Pallas kernels, shards(): call(paired_kernel, [((WIDTH, HP), BF16), ((WIDTH, 2 * N), BF16), ((WIDTH...  12.4 us
    pallas_call x1, Pallas kernels, shards(): call(front_kernel, [((2, L, HP), F32), ((2, L, 2 * N), F32), ((2, L, H),...  8.3 us
    pallas_call x1, Pallas kernels, shards(): call(grad_kernel, [((2, L, HP), BF16), ((2, 2, L, 2 * N), BF16), ((2, L,...  6.63 us
    unnamed x3, local copies, waits for them, and re-layouts  4.61 us

profile of v1, /device:TPU:6, one launch (start us, length us, event | category | flops | bytes accessed | tf_op | source)
XLA Modules:
  0.0 157.3 jit_solution(9401898517206370951)
XLA Ops:
  0.6 1.8 %copy.15.dt_weight = bf16[2048,8]{1,0:T(8,128)(2,1)} copy(bf16[2048,8]{0,1:T(8,128)(2,1)} %param.17) | data formatting | bytes 65536 | tf_op args[6]
  2.4 8.3 %shard_map.123 = (f32[2,128,512]{2,1,0:T(8,128)}, f32[2,128,256]{2,1,0:T(8,128)}, f32[2,128,8]{2,1,0:T(8,128)}, bf16[2048,128]{1,0:T(8,128)(2,1)}, f32[2,4,264,128]{3,2,1,0:T(8,128)}) custom-call(s32[1,128]{1,0:T(1,128)} %bitcast.12, bf16[128,2048]{1,0:T(8,128)(2,1)} %residual.1, s32[1,2048]{1,0:T(1,128)} %bitcast.6, bf16[12,2048]{1,0:T(8,128)(2,1)} %embedding.1, ...), custom_call_target="tpu_custom_call" | custom-call | tf_op jit(solution)/shard_map/pallas_call | solution.py:383
  10.7 91.5 %shard_map.124.states = f32[2,4,256,128]{3,2,1,0:T(8,128)} custom-call(f32[2,4,264,128]{3,2,1,0:T(8,128)} %get-tuple-element.21.sums), custom_call_target="tpu_custom_call" | custom-call | tf_op jit(solution)/shard_map/pallas_call | solution.py:394
  102.2 6.6 %shard_map.125 = (bf16[2,128,512]{2,1,0:T(8,128)(2,1)}, bf16[2,2,128,256]{3,2,1,0:T(8,128)(2,1)}, bf16[2,128,8]{2,1,0:T(8,128)(2,1)}) custom-call(f32[2,128,512]{2,1,0:T(8,128)} %get-tuple-element.18.x, f32[2,128,256]{2,1,0:T(8,128)} %get-tuple-element.19.mixed, f32[2,128,8]{2,1,0:T(8,128)} %get-tuple-element.20.pre, f32[1,8]{1,0:T(1,128)} %bitcast.9, ...), custom_call_target="tpu_custom_call" | custom-call | tf_op jit(solution)/shard_map/pallas_call | solution.py:407
  108.8 12.4 %shard_map.122 = (bf16[2048,512]{1,0:T(8,128)(2,1)}, bf16[2048,256]{1,0:T(8,128)(2,1)}, bf16[2048,8]{1,0:T(8,128)(2,1)}) custom-call(s32[1,2048]{1,0:T(1,128)} %bitcast.7, bf16[2048,512]{1,0:T(8,128)(2,1)} %x_weight.5, bf16[2048,256]{1,0:T(8,128)(2,1)} %bc_weight.5, bf16[2048,8]{1,0:T(8,128)(2,1)} %copy.15.dt_weight), custom_call_target="tpu_custom_call" | custom-call | tf_op jit(solution)/shard_map/pallas_call | solution.py:404
  121.2 33.2 %shard_map.126 = (f32[512,128]{1,0:T(8,128)}, f32[1,128]{1,0:T(1,128)}) custom-call(bf16[2048,512]{1,0:T(8,128)(2,1)} %x_weight.5, bf16[2048,256]{1,0:T(8,128)(2,1)} %bc_weight.5, bf16[2048,8]{1,0:T(8,128)(2,1)} %copy.15.dt_weight, bf16[2048,512]{1,0:T(8,128)(2,1)} %get-tuple-element.15.x_paired, bf16[2048,256]{1,0:T(8,128)(2,1)} %get-tuple-element.16.bc_paired, ...), custom_call_target="tpu_custom_call" | custom-call | tf_op jit(solution)/shard_map/pallas_call | solution.py:412
  154.4 1.7 %copy.18 = f32[512,128]{1,0:T(8,128)} copy(f32[512,128]{1,0:T(8,128)} %get-tuple-element.30) | data formatting | bytes 524288
  156.1 1.2 copy.19

commit v2 on v1

v2 whole, which is shorter than its diff:
```python
import functools
import math

import jax
import jax.numpy as jnp
from jax import lax
from jax.experimental import pallas as pl
from jax.experimental.pallas import tpu as pltpu
from jax.sharding import PartitionSpec as P

L = 128
H = 8
HP = 512
N = 128
WIDTH = 2048
TILE = 256
F32 = jnp.float32
BF16 = jnp.bfloat16
NEG = -1e30
MESH = pl.DeviceIdType.MESH

NN = (((1,), (0,)), ((), ()))
NT = (((1,), (1,)), ((), ()))
TN = (((0,), (0,)), ((), ()))


def fast(a, b, dims=NN):
    return lax.dot_general(a.astype(BF16), b.astype(BF16), dims, preferred_element_type=F32)


def parts(a, terms=3):
    held = []
    for _ in range(terms):
        held.append(a.astype(BF16))
        a = a - held[-1].astype(F32)
    return held


def split(a, b, dims=NN, right=False):
    if right:
        a, b = a.astype(BF16), parts(b)
        return sum(lax.dot_general(a, p, dims, preferred_element_type=F32) for p in b)
    b = b.astype(BF16)
    return sum(lax.dot_general(p, b, dims, preferred_element_type=F32) for p in parts(a))


def split_right(a, b):
    return split(a, b, NN, True)


def iota(shape, axis):
    return lax.broadcasted_iota(jnp.int32, shape, axis)


def head_rows():
    return (iota((H, HP), 1) // 64 == iota((H, HP), 0)).astype(F32)


def reach(branch):
    row, col = iota((L, L), 0), iota((L, L), 1)
    return col <= row if branch == 0 else col >= row


def rates(pre, bias, rate):
    z = pre + bias
    stride = jnp.maximum(z, 0.0) + jnp.log1p(jnp.exp(-jnp.abs(z)))
    return z, stride, -rate * stride


def embed(tokens_row, embedding, residual):
    vocab = embedding.shape[0]
    hot = (iota((vocab, L), 0) == tokens_row).astype(F32).T.astype(BF16)
    return (
        jnp.dot(hot, embedding, preferred_element_type=F32) + residual.astype(F32)
    ).astype(BF16)


def summaries(branch, x, mixed, pre, bias, rate, upstream):
    _, stride, log_decay = rates(pre, bias, rate)
    run = split_right(reach(branch).astype(F32), log_decay)
    total = jnp.sum(log_decay, axis=0, keepdims=True)
    spread = head_rows()
    carried = x * split(jnp.exp(total - run) * stride, spread)
    grown = upstream * split(jnp.exp(run), spread)
    end = fast(carried.T, mixed[:, :N])
    direct = fast(grown.T, mixed[:, N:])
    return jnp.exp(total), end, direct, carried, grown


def local_grads(branch, x, mixed, pre, bias, rate, skip, ups):
    writer, reader = mixed[:, :N], mixed[:, N:]
    _, stride, log_decay = rates(pre, bias, rate)
    mask_t = reach(1 - branch)
    run = split_right(reach(branch).astype(F32), log_decay)
    run_t = run.T
    spread = head_rows()
    low_half = iota((L, 2 * 64), 1) < 64
    scores_t = fast(writer, reader, NT)
    volume = jnp.zeros((L, L), F32)
    rows = []
    pieces = []
    for pair in range(H // 2):
        lanes = slice(128 * pair, 128 * pair + 128)
        x_pair, u_pair = x[:, lanes], ups[:, lanes]
        kernels, uppers = [], []
        for half in range(2):
            h = 2 * pair + half
            mine = low_half if half == 0 else jnp.logical_not(low_half)
            u_half = jnp.where(mine, u_pair, 0.0)
            fade = jnp.exp(jnp.where(mask_t, run_t[h : h + 1, :] - run[:, h : h + 1], NEG))
            cross = fast(x_pair, u_half, NT)
            weight = fade * cross * stride[:, h : h + 1]
            volume = volume + weight
            rows.append(jnp.sum(weight * scores_t, axis=0, keepdims=True))
            kernels.append((fade * scores_t).astype(BF16))
            uppers.append(u_half.astype(BF16))
        pieces.append(fast(jnp.concatenate(kernels, axis=1), jnp.concatenate(uppers, axis=0)))
    inner = jnp.concatenate(pieces, axis=1)
    d_inputs = split(skip, spread) * ups + split(stride, spread) * inner
    per_write = split(x * inner, spread.T)
    per_read = jnp.concatenate(rows, axis=0).T
    return d_inputs, fast(volume, reader), fast(volume.T, writer), per_read, per_write


def full_grads(branch, x, mixed, pre, bias, rate, carried, grown, entry, later, local):
    d_inputs, d_writer, d_reader, per_read, per_write = local
    writer, reader = mixed[:, :N], mixed[:, N:]
    z, stride, log_decay = rates(pre, bias, rate)
    run = split_right(reach(branch).astype(F32), log_decay)
    total = jnp.sum(log_decay, axis=0, keepdims=True)
    spread = head_rows()
    spread_t = spread.T
    outer = split(jnp.exp(total - run), spread) * fast(writer, later, NT)
    d_inputs = d_inputs + split(stride, spread) * outer
    d_writer = d_writer + fast(carried, later)
    d_reader = d_reader + fast(grown, entry)
    written = split(x * outer, spread_t)
    per_write = per_write + written
    per_read = per_read + split(grown * fast(reader, entry, NT), spread_t)
    dots = split_right(spread, entry * later)
    overlap = split(jnp.ones((8, L), F32), dots, NT, True)[0:1]
    d_total = jnp.exp(total) * overlap + jnp.sum(stride * written, axis=0, keepdims=True)
    d_run = per_read - stride * per_write
    d_log = split_right(reach(1 - branch).astype(F32), d_run) + d_total
    d_stride = per_write - rate * d_log
    d_pre = d_stride / (1.0 + jnp.exp(-z))
    return d_inputs, d_pre, d_writer, d_reader


def project(source, x_weight, bc_weight, dt_rows):
    dot = functools.partial(jnp.dot, preferred_element_type=F32)
    pre = lax.dot_general(source, dt_rows, NT, preferred_element_type=F32)
    return dot(source, x_weight), dot(source, bc_weight), pre


def permutation(pairing_row, first, count, axis):
    shape = (WIDTH, count) if axis == 1 else (count, WIDTH)
    return (iota(shape, 0) + (0 if axis == 1 else first) == pairing_row).astype(F32).astype(BF16)


def padded_rows(factor, first):
    wide = jnp.broadcast_to(factor, (H, H))
    own = jnp.where(iota((H, H), 0) + first == iota((H, H), 1), wide, 0.0)
    return jnp.broadcast_to(jnp.sum(own, axis=1, keepdims=True), (H, N))


def front_kernel(
    tokens, residual, pairing, embedding, x_weight, bc_weight, dt_rows, bias, rate, cotangent,
    x_out, mixed_out, pre_out, carried_out, grown_out, layer_t, sums, factors, source,
):
    layer = embed(tokens[...], embedding[...], residual[...])
    layer_t[...] = layer.astype(F32).T.astype(BF16)
    for block in range(WIDTH // TILE):
        cols = slice(TILE * block, TILE * block + TILE)
        hot = permutation(pairing[:, cols], 0, TILE, 1)
        source[:, cols] = jnp.dot(layer, hot, preferred_element_type=F32).astype(BF16)
    upstream = cotangent[...].astype(F32)
    for branch in range(2):
        read = layer if branch == 0 else source[...]
        x, mixed, pre = project(read, x_weight[...], bc_weight[...], dt_rows[...])
        x_out[branch] = x
        mixed_out[branch] = mixed
        pre_out[branch] = pre
        factor, end, direct, carried, grown = summaries(
            branch, x, mixed, pre, bias[...], rate[...], upstream
        )
        carried_out[branch] = carried.astype(BF16)
        grown_out[branch] = grown
        up, down = (end, direct) if branch == 0 else (direct, end)
        for way, value in ((0, up), (1, down)):
            for h in range(H):
                sums[way, h % 4, 2 * branch + h // 4] = value[64 * h : 64 * h + 64]
        for part in range(2):
            factors[2 * branch + part] = padded_rows(factor, 4 * part)


def scan_kernel(
    sums, factors, pairing, x_weight, bc_weight, dt_rows, x, mixed, pre, bias, rate, skip, cotangent,
    out, x_out, bc_out, dt_out, g_x, g_mixed, g_read, g_write,
    mate_in, mate_fac, chip, z_in, z_pre, x_in, y_in, e_out, e_in, far, far_in, x_fac, z_fac, send, recv,
):
    seq, head = lax.axis_index("seq"), lax.axis_index("head")
    core = lax.rem(seq, 2)
    z = lax.rem(seq // 2, 4)
    xx = lax.rem(seq // 8, 4)
    yy = seq // 32

    def device(y_at, x_at, z_at, core_at):
        return (((y_at * 4 + x_at) * 4 + z_at) * 2 + core_at, head)

    def other(value, step):
        return lax.rem(value + step, 4)

    mate = device(yy, xx, z, 1 - core)
    z_peer = [device(yy, xx, other(z, d), core) for d in (1, 2, 3)]
    x_peer = [device(yy, other(xx, d), z, core) for d in (1, 2, 3)]
    y_peer = [device(other(yy, d), xx, z, core) for d in (1, 2, 3)]
    barrier = pltpu.get_barrier_semaphore()
    for peer in [mate] + z_peer + x_peer + y_peer:
        pl.semaphore_signal(barrier, inc=1, device_id=peer, device_id_type=MESH)
    pl.semaphore_wait(barrier, 10)
    started = []

    def push(source, target, slot, peer):
        copy = pltpu.make_async_remote_copy(
            src_ref=source, dst_ref=target, send_sem=send.at[slot], recv_sem=recv.at[slot],
            device_id=peer, device_id_type=MESH,
        )
        copy.start()
        started.append(copy)
        return copy

    def place(j):
        return jnp.where(core == 0, j, 3 - j)

    def size(k):
        return pl.ds(0, 72 if k == 0 else 64)

    mate_f = push(factors, mate_fac, 0, mate)
    mate_s = [push(sums.at[1 - core, k], mate_in.at[k], 1 + k, mate) for k in range(4)]
    mate_f.wait_recv()
    z_s, x_s, y_s, e_s, far_s = [], [], [], [], []
    for k in range(4):
        mate_s[k].wait_recv()
        for q in range(4):
            chip[k, q, 0:64, :] = (
                mate_fac[q, k : k + 1, :] * sums[core, k, q] + mate_in[k, q]
            )
            if k == 0:
                chip[k, q, 64:72, :] = mate_fac[q] * factors[q]
        z_s.append([
            push(chip.at[k, other(z, d), size(k)], z_in.at[k, z, size(k)], 4 + 3 * k + d, z_peer[d - 1])
            for d in (1, 2, 3)
        ])
        z_in[k, z] = chip[k, z]

    def z_step(k):
        for copy in z_s[k]:
            copy.wait_recv()
        first = place(0)
        line = z_in[k, first, 0:64, :]
        factor = z_in[0, first, 64:72, :]
        for j in range(1, 4):
            spot = place(j)
            z_pre[k, spot] = line
            if k == 0:
                z_fac[spot] = factor
                factor = factor * z_in[0, spot, 64:72, :]
            line = z_in[0, spot, 64 + k : 65 + k, :] * line + z_in[k, spot, 0:64, :]
        x_in[k, xx, 0:64, :] = line
        if k == 0:
            x_in[k, xx, 64:72, :] = factor
        x_s.append([
            push(x_in.at[k, xx, size(k)], x_in.at[k, xx, size(k)], 16 + 3 * k + d, x_peer[d - 1])
            for d in (1, 2, 3)
        ])

    def before(held, k, mine):
        total, prefix = jnp.zeros((64, N), F32), jnp.zeros((64, N), F32)
        for j in range(4):
            spot = place(j)
            prefix = jnp.where(spot == mine, total, prefix)
            total = held[0, spot, 64 + k : 65 + k, :] * total + held[k, spot, 0:64, :]
        return prefix, total

    x_prefix = [None] * 4

    def x_step(k):
        for copy in x_s[k]:
            copy.wait_recv()
        x_prefix[k], total = before(x_in, k, xx)
        y_in[k, yy, 0:64, :] = total
        if k == 0:
            factor, prefix = jnp.ones((8, N), F32), jnp.ones((8, N), F32)
            for j in range(4):
                spot = place(j)
                prefix = jnp.where(spot == xx, factor, prefix)
                factor = factor * x_in[0, spot, 64:72, :]
            x_fac[...] = prefix
            y_in[k, yy, 64:72, :] = factor
        y_s.append([
            push(y_in.at[k, yy, size(k)], y_in.at[k, yy, size(k)], 28 + 3 * k + d, y_peer[d - 1])
            for d in (1, 2, 3)
        ])

    def y_step(k):
        for copy in y_s[k]:
            copy.wait_recv()
        y_prefix, _ = before(y_in, k, yy)
        line = x_fac[k : k + 1, :] * y_prefix + x_prefix[k]
        e_out[k, place(0)] = line
        for j in range(1, 4):
            spot = place(j)
            e_out[k, spot] = z_fac[spot, k : k + 1, :] * line + z_pre[k, spot]
        e_s.append([
            push(e_out.at[k, other(z, d)], e_in.at[k, z], 40 + 3 * k + d, z_peer[d - 1])
            for d in (1, 2, 3)
        ])
        e_in[k, z] = e_out[k, z]

    z_step(0)
    z_step(1)
    x_step(0)
    y_step(0)
    z_step(2)
    x_step(1)
    y_step(1)
    z_step(3)
    x_step(2)
    y_step(2)
    x_step(3)
    y_step(3)

    ups = cotangent[...].astype(F32)
    for branch in range(2):
        d_in, d_w, d_r, per_read, per_write = local_grads(
            branch, x[branch], mixed[branch], pre[branch], bias[...], rate[...], skip[...], ups
        )
        g_x[branch] = d_in
        g_mixed[branch, :, 0:N] = d_w
        g_mixed[branch, :, N : 2 * N] = d_r
        g_read[branch] = per_read
        g_write[branch] = per_write
    for block in range(WIDTH // TILE):
        rows = slice(TILE * block, TILE * block + TILE)
        hot = permutation(pairing[...], TILE * block, TILE, 0)
        for weight, target in ((x_weight, x_out), (bc_weight, bc_out)):
            target[rows, :] = jnp.dot(hot, weight[...], preferred_element_type=F32).astype(BF16)
        dt_out[:, rows] = lax.dot_general(
            dt_rows[...], hot, NT, preferred_element_type=F32
        ).astype(BF16)

    for k in range(4):
        for copy in e_s[k]:
            copy.wait_recv()
        for q in range(4):
            far[k, q] = factors[q, k : k + 1, :] * e_in[k, q] + sums[core, k, q]
            out[core, k, q] = e_in[k, q]
        far_s.append(push(far.at[k], far_in.at[k], 53 + k, mate))
    for k in range(4):
        far_s[k].wait_recv()
        out[1 - core, k] = far_in[k]
    for copy in started:
        copy.wait_send()


def back_kernel(
    x_weight, bc_weight, dt_rows, x_paired, bc_paired, dt_paired, x, mixed, pre, bias, rate,
    carried, grown, states, g_x, g_mixed, g_read, g_write, layer_t,
    grad, saliency, part, got, d_x, d_mixed, d_pre, sal_part, sal_got, send, recv,
):
    seq, head = lax.axis_index("seq"), lax.axis_index("head")

    def peer(index):
        return (seq, index)

    barrier = pltpu.get_barrier_semaphore()
    for step in (1, 2, 3):
        pl.semaphore_signal(barrier, inc=1, device_id=peer(lax.rem(head + step, 4)), device_id_type=MESH)
    pl.semaphore_wait(barrier, 3)
    for branch in range(2):
        way = (0, 1) if branch == 0 else (1, 0)

        def whole(direction):
            return jnp.concatenate(
                [states[direction, h % 4, 2 * branch + h // 4] for h in range(H)], axis=0
            )

        local = (
            g_x[branch], g_mixed[branch, :, 0:N], g_mixed[branch, :, N : 2 * N], g_read[branch],
            g_write[branch],
        )
        full_x, full_pre, g_writer, g_reader = full_grads(
            branch, x[branch], mixed[branch], pre[branch], bias[...], rate[...], carried[branch],
            grown[branch], whole(way[0]), whole(way[1]), local,
        )
        d_x[branch] = full_x.astype(BF16)
        d_pre[branch] = full_pre.astype(BF16)
        for column, value in ((0, g_writer), (N, g_reader)):
            high = value.astype(BF16)
            d_mixed[branch, 0, :, column : column + N] = high
            d_mixed[branch, 1, :, column : column + N] = (value - high.astype(F32)).astype(BF16)
    rows_here = WIDTH // 4

    def push(source, target, sent, slot, device):
        copy = pltpu.make_async_remote_copy(
            src_ref=source, dst_ref=target, send_sem=send.at[sent], recv_sem=recv.at[slot],
            device_id=device, device_id_type=MESH,
        )
        copy.start()
        return copy

    def chunk(owner):
        first = pl.multiple_of(owner * rows_here, rows_here)
        rows = pl.ds(first, rows_here)
        total = jnp.zeros((rows_here, L), F32)
        for branch, weights in (
            (0, (x_weight, bc_weight, dt_rows)),
            (1, (x_paired, bc_paired, dt_paired)),
        ):
            total = total + lax.dot_general(weights[0][rows, :], d_x[branch], NT, preferred_element_type=F32)
            for term in range(2):
                total = total + lax.dot_general(
                    weights[1][rows, :], d_mixed[branch, term], NT, preferred_element_type=F32
                )
            dt_cols = weights[2][:, rows].astype(F32).T.astype(BF16)
            total = total + lax.dot_general(dt_cols, d_pre[branch], NT, preferred_element_type=F32)
        weighed = jnp.sum(total * layer_t[rows, :].astype(F32), axis=0, keepdims=True)
        return total, weighed

    edge = jnp.logical_or(head == 0, head == 3)
    near = jnp.where(head < 2, 1, 2)
    second = jnp.where(head == 0, 2, jnp.where(head == 1, 0, jnp.where(head == 2, 3, 1)))
    third = jnp.where(head == 0, 1, jnp.where(head == 1, 3, jnp.where(head == 2, 0, 2)))
    total, weighed = chunk(3 - head)
    part[0] = total
    to_first = jnp.where(edge, near, 3 - head)
    slot = jnp.where(edge, 0, 1)
    copies = [push(part.at[0], got.at[slot], 0, slot, peer(to_first))]
    total, share = chunk(second)
    weighed = weighed + share
    part[1] = total
    copies.append(push(part.at[1], got.at[2], 1, 2, peer(second)))
    total, share = chunk(third)
    weighed = weighed + share
    part[2] = total

    def arrived(index):
        pltpu.make_async_remote_copy(
            src_ref=part.at[0], dst_ref=got.at[index], send_sem=send.at[0], recv_sem=recv.at[index],
            device_id=peer(3 - head), device_id_type=MESH,
        ).wait_recv()

    @pl.when(jnp.logical_not(edge))
    def _():
        arrived(0)
        part[2] = part[2] + got[0]

    copies.append(push(part.at[2], got.at[3], 2, 3, peer(third)))
    total, share = chunk(head)
    weighed = weighed + share
    grad[...] = total
    sal_part[...] = jnp.broadcast_to(weighed, (8, L))
    sal_got[head] = sal_part[...]
    shares = [
        push(sal_part, sal_got.at[head], 2 + step, 3 + step, peer(lax.rem(head + step, 4)))
        for step in (1, 2, 3)
    ]
    for copy in shares:
        copy.wait_recv()
    saliency[...] = (
        ((sal_got[0, 0:1] + sal_got[1, 0:1]) + sal_got[2, 0:1]) + sal_got[3, 0:1]
    ) / math.sqrt(WIDTH)

    @pl.when(jnp.logical_not(edge))
    def _():
        arrived(1)
        grad[...] = grad[...] + got[1]

    arrived(2)
    grad[...] = grad[...] + got[2]
    arrived(3)
    grad[...] = grad[...] + got[3]
    for copy in copies + shares:
        copy.wait_send()


VM = pl.BlockSpec(memory_space=pltpu.VMEM)


def call(kernel, outs, count, scratch=(), comm=None):
    return pl.pallas_call(
        kernel,
        out_shape=[jax.ShapeDtypeStruct(shape, dtype) for shape, dtype in outs],
        in_specs=[VM] * count,
        out_specs=[VM] * len(outs),
        scratch_shapes=list(scratch),
        compiler_params=pltpu.CompilerParams(
            collective_id=comm, has_side_effects=comm is not None, vmem_limit_bytes=60 << 20
        ),
    )


def shards(
    tokens, residual_in, pairing, embedding, x_weight, bc_weight, dt_weight, dt_bias, decay_rate,
    skip_gain, cotangent,
):
    tokens_row, pairing_row = tokens.reshape(1, L), pairing.reshape(1, WIDTH)
    bias, rate, skip = (value.reshape(1, H) for value in (dt_bias, decay_rate, skip_gain))
    dt_rows = dt_weight.T
    x, mixed, pre, carried, grown, layer_t, sums, factors = call(
        front_kernel,
        [
            ((2, L, HP), F32), ((2, L, 2 * N), F32), ((2, L, H), F32), ((2, L, HP), BF16),
            ((2, L, HP), F32), ((WIDTH, L), BF16), ((2, 4, 4, 64, N), F32), ((4, 8, N), F32),
        ],
        10,
        [pltpu.VMEM((L, WIDTH), BF16)],
    )(tokens_row, residual_in, pairing_row, embedding, x_weight, bc_weight, dt_rows, bias, rate, cotangent)
    plain = pltpu.VMEM((4, 4, 64, N), F32)
    tall = pltpu.VMEM((4, 4, 72, N), F32)
    states, x_paired, bc_paired, dt_paired, g_x, g_mixed, g_read, g_write = call(
        scan_kernel,
        [
            ((2, 4, 4, 64, N), F32), ((WIDTH, HP), BF16), ((WIDTH, 2 * N), BF16), ((H, WIDTH), BF16),
            ((2, L, HP), F32), ((2, L, 2 * N), F32), ((2, L, H), F32), ((2, L, H), F32),
        ],
        13,
        [
            plain, pltpu.VMEM((4, 8, N), F32), tall, tall, plain, tall, tall, plain, plain, plain, plain,
            pltpu.VMEM((8, N), F32), pltpu.VMEM((4, 8, N), F32), pltpu.SemaphoreType.DMA((57,)),
            pltpu.SemaphoreType.DMA((57,)),
        ],
        comm=0,
    )(sums, factors, pairing_row, x_weight, bc_weight, dt_rows, x, mixed, pre, bias, rate, skip, cotangent)
    grad, saliency = call(
        back_kernel,
        [((WIDTH // 4, L), F32), ((1, L), F32)],
        19,
        [
            pltpu.VMEM((3, WIDTH // 4, L), F32), pltpu.VMEM((4, WIDTH // 4, L), F32),
            pltpu.VMEM((2, L, HP), BF16), pltpu.VMEM((2, 2, L, 2 * N), BF16), pltpu.VMEM((2, L, H), BF16),
            pltpu.VMEM((8, L), F32), pltpu.VMEM((4, 8, L), F32),
            pltpu.SemaphoreType.DMA((6,)), pltpu.SemaphoreType.DMA((7,)),
        ],
        comm=1,
    )(
        x_weight, bc_weight, dt_rows, x_paired, bc_paired, dt_paired, x, mixed, pre, bias, rate,
        carried, grown, states, g_x, g_mixed, g_read, g_write, layer_t,
    )
    return grad, saliency.reshape(L)


def solution(mesh):
    return jax.shard_map(
        shards,
        mesh=mesh,
        in_specs=(
            P("seq"), P("seq", None), P(), P(), P(None, "head"), P(), P(None, "head"), P("head"),
            P("head"), P("head"), P("seq", "head"),
        ),
        out_specs=(P("head", "seq"), P("seq")),
        check_vma=False,
    )
```

time: 158 us -> 120 us (0.76)
  Pallas kernels: 152 us -> 115 us
  local copies, waits for them, and re-layouts: 4.61 us -> 2.79 us
    pallas_call x4 -> x2, Pallas kernels: 144 us -> 108 us  [the longest x1 68.7 us: shards(): call(scan_kernel, [((2, 4, 4, 64, N), F32), ((WIDTH, HP), BF16), ((WIDTH,...]
    unnamed x3 -> x2, local copies, waits for them, and re-layouts: 4.61 us -> 2.79 us
where the time goes in v2:
time: 120 us; the launch traced here: 119 us
  Pallas kernels  115 us (96%)
  local copies, waits for them, and re-layouts  2.79 us (2%)
    pallas_call x1, Pallas kernels, shards(): call(scan_kernel, [((2, 4, 4, 64, N), F32), ((WIDTH, HP), BF16), ((WIDTH,...  68.7 us
    pallas_call x1, Pallas kernels, shards(): call(back_kernel, [((WIDTH // 4, L), F32), ((1, L), F32)], 19, [pltpu.VME...  39.1 us
    pallas_call x1, Pallas kernels, shards(): call(front_kernel, [((2, L, HP), F32), ((2, L, 2 * N), F32), ((2, L, H),...  7.35 us
    unnamed x2, local copies, waits for them, and re-layouts  2.79 us

profile of v2, /device:TPU:6, one launch (start us, length us, event | category | flops | bytes accessed | tf_op | source)
XLA Modules:
  0.0 118.6 jit_solution(16300668859836076013)
XLA Ops:
  0.6 7.3 %shard_map.122 = (f32[2,128,512]{2,1,0:T(8,128)}, f32[2,128,256]{2,1,0:T(8,128)}, f32[2,128,8]{2,1,0:T(8,128)}, bf16[2,128,512]{2,1,0:T(8,128)(2,1)}, f32[2,128,...) custom-call(s32[1,128]{1,0:T(1,128)} %bitcast.18, ...), custom_call_target="tpu_custom_call" | custom-call | tf_op jit(solution)/shard_map/pallas_call | solution.py:511
  8.0 68.7 %shard_map.123 = (f32[2,4,4,64,128]{4,3,2,1,0:T(8,128)}, bf16[2048,512]{1,0:T(8,128)(2,1)}, bf16[2048,256]{1,0:T(8,128)(2,1)}, bf16[8,2048]{1,0:T(8,128)(2,1)}, ...) custom-call(f32[2,4,4,64,128]{4,3,2,1,0:T(8,128)} %get-tuple-element.20.sums, ...), custom_call_target="tpu_custom_call" | custom-call | tf_op jit(solution)/shard_map/pallas_call | solution.py:522
  76.7 39.1 %shard_map.124 = (f32[512,128]{1,0:T(8,128)}, f32[1,128]{1,0:T(1,128)}) custom-call(bf16[2048,512]{1,0:T(8,128)(2,1)} %x_weight.5, bf16[2048,256]{1,0:T(8,128)(2,1)} %bc_weight.5, bf16[8,2048]{1,0:T(8,128)(2,1)} %bitcast.9, bf16[2048,512]{1,0:T(8,128)(2,1)} %get-tuple-element.25.x_paired, bf16[2048,256]{1,0:T(8,128)(2,1)} %get-tuple-element.26.bc_paired, ...), custom_call_target="tpu_custom_call" | custom-call | tf_op jit(solution)/shard_map/pallas_call | solution.py:536
  115.8 1.7 %copy.15 = f32[512,128]{1,0:T(8,128)} copy(f32[512,128]{1,0:T(8,128)} %get-tuple-element.40) | data formatting | bytes 524288
  117.5 1.1 copy.16

commit v3 on v2

v3 whole, which is shorter than its diff:
```python
import functools
import math

import jax
import jax.numpy as jnp
from jax import lax
from jax.experimental import pallas as pl
from jax.experimental.pallas import tpu as pltpu
from jax.sharding import PartitionSpec as P

L = 128
H = 8
HP = 512
N = 128
WIDTH = 2048
TILE = 256
F32 = jnp.float32
BF16 = jnp.bfloat16
NEG = -1e30
MESH = pl.DeviceIdType.MESH

NN = (((1,), (0,)), ((), ()))
NT = (((1,), (1,)), ((), ()))
TN = (((0,), (0,)), ((), ()))


def fast(a, b, dims=NN):
    return lax.dot_general(a.astype(BF16), b.astype(BF16), dims, preferred_element_type=F32)


def parts(a, terms=3):
    held = []
    for _ in range(terms):
        held.append(a.astype(BF16))
        a = a - held[-1].astype(F32)
    return held


def split(a, b, dims=NN, right=False):
    if right:
        a, b = a.astype(BF16), parts(b)
        return sum(lax.dot_general(a, p, dims, preferred_element_type=F32) for p in b)
    b = b.astype(BF16)
    return sum(lax.dot_general(p, b, dims, preferred_element_type=F32) for p in parts(a))


def split_right(a, b):
    return split(a, b, NN, True)


def iota(shape, axis):
    return lax.broadcasted_iota(jnp.int32, shape, axis)


def head_rows():
    return (iota((H, HP), 1) // 64 == iota((H, HP), 0)).astype(F32)


def reach(branch):
    row, col = iota((L, L), 0), iota((L, L), 1)
    return col <= row if branch == 0 else col >= row


def rates(pre, bias, rate):
    z = pre + bias
    stride = jnp.maximum(z, 0.0) + jnp.log1p(jnp.exp(-jnp.abs(z)))
    return z, stride, -rate * stride


def embed(tokens_row, embedding, residual):
    vocab = embedding.shape[0]
    hot = (iota((vocab, L), 0) == tokens_row).astype(F32).T.astype(BF16)
    return (
        jnp.dot(hot, embedding, preferred_element_type=F32) + residual.astype(F32)
    ).astype(BF16)


def local_grads(branch, x, mixed, stride, run, skip, ups):
    writer, reader = mixed[:, :N], mixed[:, N:]
    mask_t = reach(1 - branch)
    run_t = run.T
    spread = head_rows()
    low_half = iota((L, 2 * 64), 1) < 64
    scores_t = fast(writer, reader, NT)
    volume = jnp.zeros((L, L), F32)
    rows = []
    pieces = []
    for pair in range(H // 2):
        lanes = slice(128 * pair, 128 * pair + 128)
        x_pair, u_pair = x[:, lanes], ups[:, lanes]
        kernels, uppers = [], []
        for half in range(2):
            h = 2 * pair + half
            mine = low_half if half == 0 else jnp.logical_not(low_half)
            u_half = jnp.where(mine, u_pair, 0.0)
            fade = jnp.exp(jnp.where(mask_t, run_t[h : h + 1, :] - run[:, h : h + 1], NEG))
            cross = fast(x_pair, u_half, NT)
            weight = fade * cross * stride[:, h : h + 1]
            volume = volume + weight
            rows.append(jnp.sum(weight * scores_t, axis=0, keepdims=True))
            kernels.append((fade * scores_t).astype(BF16))
            uppers.append(u_half.astype(BF16))
        pieces.append(fast(jnp.concatenate(kernels, axis=1), jnp.concatenate(uppers, axis=0)))
    inner = jnp.concatenate(pieces, axis=1)
    d_inputs = split(skip, spread) * ups + split(stride, spread) * inner
    per_write = split(x * inner, spread.T)
    per_read = jnp.concatenate(rows, axis=0).T
    return d_inputs, fast(volume, reader), fast(volume.T, writer), per_read, per_write


def full_grads(
    branch, x, mixed, z, stride, run, rate, stride_e, decay_e, carried, grown, entry, later, local
):
    d_inputs, d_writer, d_reader, per_read, per_write = local
    writer, reader = mixed[:, :N], mixed[:, N:]
    total = run[L - 1 : L] if branch == 0 else run[0:1]
    spread = head_rows()
    spread_t = spread.T
    outer = decay_e * fast(writer, later, NT)
    d_inputs = d_inputs + stride_e * outer
    d_writer = d_writer + fast(carried, later)
    d_reader = d_reader + fast(grown, entry)
    written = split(x * outer, spread_t)
    per_write = per_write + written
    per_read = per_read + split(grown * fast(reader, entry, NT), spread_t)
    dots = split_right(spread, entry * later)
    overlap = split(jnp.ones((8, L), F32), dots, NT, True)[0:1]
    d_total = jnp.exp(total) * overlap + jnp.sum(stride * written, axis=0, keepdims=True)
    d_run = per_read - stride * per_write
    d_log = split_right(reach(1 - branch).astype(F32), d_run) + d_total
    d_stride = per_write - rate * d_log
    d_pre = d_stride / (1.0 + jnp.exp(-z))
    return d_inputs, d_pre, d_writer, d_reader


def project(source, x_weight, bc_weight, dt_rows):
    dot = functools.partial(jnp.dot, preferred_element_type=F32)
    pre = lax.dot_general(source, dt_rows, NT, preferred_element_type=F32)
    return dot(source, x_weight), dot(source, bc_weight), pre


def permutation(pairing_row, first, count, axis):
    shape = (WIDTH, count) if axis == 1 else (count, WIDTH)
    return (iota(shape, 0) + (0 if axis == 1 else first) == pairing_row).astype(F32).astype(BF16)


def padded_rows(factor, first):
    wide = jnp.broadcast_to(factor, (H, H))
    own = jnp.where(iota((H, H), 0) + first == iota((H, H), 1), wide, 0.0)
    return jnp.broadcast_to(jnp.sum(own, axis=1, keepdims=True), (H, N))


def kernel(
    tokens, residual, pairing, embedding, x_weight, bc_weight, dt_rows, bias, rate, skip, cotangent,
    grad, saliency,
    source, layer_t, ups, x, mixed, zs, strides, runs, stride_e, decay_e, carried, grown,
    g_x, g_mixed, g_read, g_write, x_paired, bc_paired, dt_paired,
    sums, factors, mate_in, mate_fac, chip, z_in, z_pre, x_in, y_in, e_out, e_in, far, far_in,
    x_fac, z_fac, states, d_x, d_mixed, d_pre, forward, part, got, sal_part, sal_got,
    send, recv, send_back, recv_back,
):
    seq, head = lax.axis_index("seq"), lax.axis_index("head")
    core = lax.rem(seq, 2)
    z = lax.rem(seq // 2, 4)
    xx = lax.rem(seq // 8, 4)
    yy = seq // 32

    def device(y_at, x_at, z_at, core_at):
        return (((y_at * 4 + x_at) * 4 + z_at) * 2 + core_at, head)

    def other(value, step):
        return lax.rem(value + step, 4)

    mate = device(yy, xx, z, 1 - core)
    z_peer = [device(yy, xx, other(z, d), core) for d in (1, 2, 3)]
    x_peer = [device(yy, other(xx, d), z, core) for d in (1, 2, 3)]
    y_peer = [device(other(yy, d), xx, z, core) for d in (1, 2, 3)]
    h_peer = [(seq, other(head, d)) for d in (1, 2, 3)]
    barrier = pltpu.get_barrier_semaphore()
    for peer in [mate] + z_peer + x_peer + y_peer + h_peer:
        pl.semaphore_signal(barrier, inc=1, device_id=peer, device_id_type=MESH)
    started = []

    def push(source_ref, target, slot, peer):
        copy = pltpu.make_async_remote_copy(
            src_ref=source_ref, dst_ref=target, send_sem=send.at[slot], recv_sem=recv.at[slot],
            device_id=peer, device_id_type=MESH,
        )
        copy.start()
        started.append(copy)
        return copy

    def place(j):
        return jnp.where(core == 0, j, 3 - j)

    def size(k):
        return pl.ds(0, 72 if k % 2 == 0 else 64)

    def front(branch, read):
        x_here, mixed_here, pre = project(read, x_weight[...], bc_weight[...], dt_rows[...])
        z_here, stride, log_decay = rates(pre, bias[...], rate[...])
        run = split_right(reach(branch).astype(F32), log_decay)
        total = jnp.sum(log_decay, axis=0, keepdims=True)
        spread = head_rows()
        fade = jnp.exp(total - run)
        x[branch] = x_here
        mixed[branch] = mixed_here
        zs[branch], strides[branch], runs[branch] = z_here, stride, run
        carry = x_here * split(fade * stride, spread)
        grow = ups[...] * split(jnp.exp(run), spread)
        end = fast(carry.T, mixed_here[:, :N])
        direct = fast(grow.T, mixed_here[:, N:])
        carried[branch] = carry.astype(BF16)
        grown[branch] = grow
        up, down = (end, direct) if branch == 0 else (direct, end)
        for way, value in ((0, up), (1, down)):
            for h in range(H):
                sums[way, 2 * branch + h % 2, h // 2] = value[64 * h : 64 * h + 64]
        for q in range(4):
            factors[branch, q] = padded_rows(jnp.exp(total), 2 * q)

    z_s, x_s, y_s, e_s, far_s = {}, {}, {}, {}, {}

    def pair(branch):
        ks = (2 * branch, 2 * branch + 1)
        mate_f = push(factors.at[branch], mate_fac.at[branch], branch, mate)
        mate_s = [push(sums.at[1 - core, k], mate_in.at[k], 2 + k, mate) for k in ks]
        mate_f.wait_recv()
        for k, arriving in zip(ks, mate_s):
            arriving.wait_recv()
            row = k % 2
            for q in range(4):
                chip[k, q, 0:64, :] = (
                    mate_fac[branch, q, row : row + 1, :] * sums[core, k, q] + mate_in[k, q]
                )
                if row == 0:
                    chip[k, q, 64:72, :] = mate_fac[branch, q] * factors[branch, q]
            z_s[k] = [
                push(chip.at[k, other(z, d), size(k)], z_in.at[k, z, size(k)], 5 + 3 * k + d, z_peer[d - 1])
                for d in (2, 1, 3)
            ]
            z_in[k, z] = chip[k, z]

    def z_step(k):
        for copy in z_s[k]:
            copy.wait_recv()
        even, row = k - k % 2, k % 2
        first = place(0)
        line = z_in[k, first, 0:64, :]
        factor = z_in[even, first, 64:72, :]
        for j in range(1, 4):
            spot = place(j)
            z_pre[k, spot] = line
            if row == 0:
                z_fac[k // 2, spot] = factor
                factor = factor * z_in[k, spot, 64:72, :]
            line = z_in[even, spot, 64 + row : 65 + row, :] * line + z_in[k, spot, 0:64, :]
        x_in[k, xx, 0:64, :] = line
        if row == 0:
            x_in[k, xx, 64:72, :] = factor
        x_s[k] = [
            push(x_in.at[k, xx, size(k)], x_in.at[k, xx, size(k)], 17 + 3 * k + d, x_peer[d - 1])
            for d in (1, 2, 3)
        ]

    def before(held, k, mine):
        even, row = k - k % 2, k % 2
        total, prefix = jnp.zeros((64, N), F32), jnp.zeros((64, N), F32)
        for j in range(4):
            spot = place(j)
            prefix = jnp.where(spot == mine, total, prefix)
            total = held[even, spot, 64 + row : 65 + row, :] * total + held[k, spot, 0:64, :]
        return prefix, total

    x_prefix = {}

    def x_step(k):
        for copy in x_s[k]:
            copy.wait_recv()
        x_prefix[k], total = before(x_in, k, xx)
        y_in[k, yy, 0:64, :] = total
        if k % 2 == 0:
            factor, prefix = jnp.ones((8, N), F32), jnp.ones((8, N), F32)
            for j in range(4):
                spot = place(j)
                prefix = jnp.where(spot == xx, factor, prefix)
                factor = factor * x_in[k, spot, 64:72, :]
            x_fac[k // 2] = prefix
            y_in[k, yy, 64:72, :] = factor
        y_s[k] = [
            push(y_in.at[k, yy, size(k)], y_in.at[k, yy, size(k)], 29 + 3 * k + d, y_peer[d - 1])
            for d in (1, 2, 3)
        ]

    def y_step(k):
        for copy in y_s[k]:
            copy.wait_recv()
        group, row = k // 2, k % 2
        y_prefix, _ = before(y_in, k, yy)
        line = x_fac[group, row : row + 1, :] * y_prefix + x_prefix[k]
        e_out[k, place(0)] = line
        for j in range(1, 4):
            spot = place(j)
            e_out[k, spot] = z_fac[group, spot, row : row + 1, :] * line + z_pre[k, spot]
        e_s[k] = [
            push(e_out.at[k, other(z, d)], e_in.at[k, z], 41 + 3 * k + d, z_peer[d - 1])
            for d in (2, 1, 3)
        ]
        e_in[k, z] = e_out[k, z]

    def alone(branch):
        d_in, d_w, d_r, per_read, per_write = local_grads(
            branch, x[branch], mixed[branch], strides[branch], runs[branch], skip[...], ups[...]
        )
        g_x[branch] = d_in
        g_mixed[branch, :, 0:N] = d_w
        g_mixed[branch, :, N : 2 * N] = d_r
        g_read[branch] = per_read
        g_write[branch] = per_write
        spread = head_rows()
        stride_e[branch] = split(strides[branch], spread)
        run = runs[branch]
        last = run[L - 1 : L] if branch == 0 else run[0:1]
        decay_e[branch] = split(jnp.exp(last - run), spread)

    def unpair(branch):
        ks = (2 * branch, 2 * branch + 1)
        for k in ks:
            for copy in e_s[k]:
                copy.wait_recv()
            row = k % 2
            for q in range(4):
                far[k, q] = factors[branch, q, row : row + 1, :] * e_in[k, q] + sums[core, k, q]
            far_s[k] = push(far.at[k], far_in.at[k], 54 + k, mate)
            states[core, k] = e_in[k]
        for k in ks:
            far_s[k].wait_recv()
            states[1 - core, k] = far_in[k]

    def joined(branch):
        way = (0, 1) if branch == 0 else (1, 0)

        def whole(direction):
            return jnp.concatenate(
                [states[direction, 2 * branch + h % 2, h // 2] for h in range(H)], axis=0
            )

        local = (
            g_x[branch], g_mixed[branch, :, 0:N], g_mixed[branch, :, N : 2 * N], g_read[branch],
            g_write[branch],
        )
        full_x, full_pre, g_writer, g_reader = full_grads(
            branch, x[branch], mixed[branch], zs[branch], strides[branch], runs[branch], rate[...],
            stride_e[branch], decay_e[branch], carried[branch], grown[branch], whole(way[0]),
            whole(way[1]), local,
        )
        d_x[branch] = full_x.astype(BF16)
        d_pre[branch] = full_pre.astype(BF16)
        for column, value in ((0, g_writer), (N, g_reader)):
            high = value.astype(BF16)
            d_mixed[branch, 0, :, column : column + N] = high
            d_mixed[branch, 1, :, column : column + N] = (value - high.astype(F32)).astype(BF16)

    def back(branch, weights, rows):
        dt_cols = weights[2][:, rows].astype(F32).T.astype(BF16)
        total = lax.dot_general(weights[0][rows, :], d_x[branch], NT, preferred_element_type=F32)
        for term in range(2):
            total = total + lax.dot_general(
                weights[1][rows, :], d_mixed[branch, term], NT, preferred_element_type=F32
            )
        return total + lax.dot_general(dt_cols, d_pre[branch], NT, preferred_element_type=F32)

    layer = embed(tokens[...], embedding[...], residual[...])
    ups[...] = cotangent[...].astype(F32)
    front(0, layer)
    pl.semaphore_wait(barrier, 13)
    pair(0)
    for block in range(WIDTH // TILE):
        cols = slice(TILE * block, TILE * block + TILE)
        hot = permutation(pairing[:, cols], 0, TILE, 1)
        source[:, cols] = jnp.dot(layer, hot, preferred_element_type=F32).astype(BF16)
    front(1, source[...])
    pair(1)
    @pl.loop(0, WIDTH // TILE)
    def _(block):
        rows = pl.ds(pl.multiple_of(block * TILE, TILE), TILE)
        hot = permutation(pairing[...], block * TILE, TILE, 0)
        for weight, target in ((x_weight, x_paired), (bc_weight, bc_paired)):
            target[rows, :] = jnp.dot(hot, weight[...], preferred_element_type=F32).astype(BF16)
        dt_paired[:, rows] = lax.dot_general(
            dt_rows[...], hot, NT, preferred_element_type=F32
        ).astype(BF16)

    z_step(0)
    z_step(1)
    x_step(0)
    y_step(0)
    z_step(2)
    x_step(1)
    y_step(1)
    z_step(3)
    x_step(2)
    y_step(2)
    x_step(3)
    y_step(3)
    layer_t[...] = layer.astype(F32).T.astype(BF16)
    alone(0)
    alone(1)
    unpair(0)
    joined(0)
    rows_here = WIDTH // 4
    for block in range(4):
        rows = slice(rows_here * block, rows_here * block + rows_here)
        forward[rows, :] = back(0, (x_weight, bc_weight, dt_rows), rows)
    unpair(1)
    joined(1)

    def chunk(owner):
        rows = pl.ds(pl.multiple_of(owner * rows_here, rows_here), rows_here)
        total = forward[rows, :] + back(1, (x_paired, bc_paired, dt_paired), rows)
        weighed = jnp.sum(total * layer_t[rows, :].astype(F32), axis=0, keepdims=True)
        return total, weighed

    def handover(source_ref, target, sent, slot, index):
        return pltpu.make_async_remote_copy(
            src_ref=source_ref, dst_ref=target, send_sem=send_back.at[sent], recv_sem=recv_back.at[slot],
            device_id=(seq, index), device_id_type=MESH,
        )

    def give(*route):
        copy = handover(*route)
        copy.start()
        started.append(copy)
        return copy

    def arrived(index):
        pltpu.make_async_remote_copy(
            src_ref=part.at[0], dst_ref=got.at[index], send_sem=send_back.at[0],
            recv_sem=recv_back.at[index], device_id=(seq, 3 - head), device_id_type=MESH,
        ).wait_recv()

    edge = jnp.logical_or(head == 0, head == 3)
    near = jnp.where(head < 2, 1, 2)
    second = jnp.where(head == 0, 2, jnp.where(head == 1, 0, jnp.where(head == 2, 3, 1)))
    third = jnp.where(head == 0, 1, jnp.where(head == 1, 3, jnp.where(head == 2, 0, 2)))
    slot = jnp.where(edge, 0, 1)
    total, weighed = chunk(3 - head)
    part[0] = total
    give(part.at[0], got.at[slot], 0, slot, jnp.where(edge, near, 3 - head))
    total, share = chunk(second)
    weighed = weighed + share
    part[1] = total
    give(part.at[1], got.at[2], 1, 2, second)
    total, share = chunk(third)
    weighed = weighed + share
    part[2] = total

    @pl.when(edge)
    def _():
        handover(part.at[2], got.at[3], 2, 3, third).start()

    total, share = chunk(head)
    weighed = weighed + share
    grad[...] = total
    sal_part[...] = jnp.broadcast_to(weighed, (8, L))
    sal_got[head] = sal_part[...]
    scan_sends = list(started[:-2])
    del started[:-2]
    shares = [
        give(sal_part, sal_got.at[head], 2 + d, 3 + d, h_peer[d - 1][1]) for d in (1, 2, 3)
    ]

    @pl.when(jnp.logical_not(edge))
    def _():
        arrived(0)
        part[2] = part[2] + got[0]
        handover(part.at[2], got.at[3], 2, 3, third).start()

    for copy in scan_sends:
        copy.wait_send()
    for copy in shares:
        copy.wait_recv()
    saliency[...] = (
        ((sal_got[0, 0:1] + sal_got[1, 0:1]) + sal_got[2, 0:1]) + sal_got[3, 0:1]
    ) / math.sqrt(WIDTH)

    @pl.when(jnp.logical_not(edge))
    def _():
        arrived(1)
        grad[...] = grad[...] + got[1]

    arrived(2)
    grad[...] = grad[...] + got[2]
    arrived(3)
    grad[...] = grad[...] + got[3]
    handover(part.at[2], got.at[3], 2, 3, third).wait_send()
    for copy in started:
        copy.wait_send()


VM = pl.BlockSpec(memory_space=pltpu.VMEM)


def final_kernel(grad, saliency, grad_out, saliency_out):
    grad_out[...] = grad[...]
    saliency_out[...] = saliency[...]


def shards(
    tokens, residual_in, pairing, embedding, x_weight, bc_weight, dt_weight, dt_bias, decay_rate,
    skip_gain, cotangent,
):
    tokens_row, pairing_row = tokens.reshape(1, L), pairing.reshape(1, WIDTH)
    bias, rate, skip = (value.reshape(1, H) for value in (dt_bias, decay_rate, skip_gain))
    shapes = [
        ((L, WIDTH), BF16), ((WIDTH, L), BF16), ((L, HP), F32), ((2, L, HP), F32),
        ((2, L, 2 * N), F32), ((2, L, H), F32), ((2, L, H), F32), ((2, L, H), F32),
        ((2, L, HP), F32), ((2, L, HP), F32), ((2, L, HP), BF16), ((2, L, HP), F32),
        ((2, L, HP), F32), ((2, L, 2 * N), F32), ((2, L, H), F32), ((2, L, H), F32),
        ((WIDTH, HP), BF16), ((WIDTH, 2 * N), BF16), ((H, WIDTH), BF16),
        ((2, 4, 4, 64, N), F32), ((2, 4, 8, N), F32), ((4, 4, 64, N), F32), ((2, 4, 8, N), F32),
        ((4, 4, 72, N), F32), ((4, 4, 72, N), F32), ((4, 4, 64, N), F32), ((4, 4, 72, N), F32),
        ((4, 4, 72, N), F32), ((4, 4, 64, N), F32), ((4, 4, 64, N), F32), ((4, 4, 64, N), F32),
        ((4, 4, 64, N), F32), ((2, 8, N), F32), ((2, 4, 8, N), F32), ((2, 4, 4, 64, N), F32),
        ((2, L, HP), BF16), ((2, 2, L, 2 * N), BF16), ((2, L, H), BF16), ((WIDTH, L), F32),
        ((3, WIDTH // 4, L), F32), ((4, WIDTH // 4, L), F32), ((8, L), F32), ((4, 8, L), F32),
    ]
    dma = pltpu.SemaphoreType.DMA
    grad, saliency = pl.pallas_call(
        kernel,
        out_shape=[
            jax.ShapeDtypeStruct((WIDTH // 4, L), F32), jax.ShapeDtypeStruct((1, L), F32),
        ],
        in_specs=[VM] * 11,
        out_specs=[VM] * 2,
        scratch_shapes=[pltpu.VMEM(*shape) for shape in shapes]
        + [dma((58,)), dma((58,)), dma((6,)), dma((7,))],
        compiler_params=pltpu.CompilerParams(
            collective_id=0, has_side_effects=True, vmem_limit_bytes=60 << 20
        ),
    )(
        tokens_row, residual_in, pairing_row, embedding, x_weight, bc_weight, dt_weight.T, bias, rate,
        skip, cotangent,
    )
    grad, saliency = pl.pallas_call(
        final_kernel,
        out_shape=[
            jax.ShapeDtypeStruct((WIDTH // 4, L), F32), jax.ShapeDtypeStruct((1, L), F32),
        ],
        in_specs=[VM] * 2,
        out_specs=[VM] * 2,
        compiler_params=pltpu.CompilerParams(vmem_limit_bytes=60 << 20),
    )(grad, saliency)
    return grad, saliency.reshape(L)


def solution(mesh):
    return jax.shard_map(
        shards,
        mesh=mesh,
        in_specs=(
            P("seq"), P("seq", None), P(), P(), P(None, "head"), P(), P(None, "head"), P("head"),
            P("head"), P("head"), P("seq", "head"),
        ),
        out_specs=(P("head", "seq"), P("seq")),
        check_vma=False,
    )
```

time: 120 us -> 96.1 us (0.80)
  Pallas kernels: 115 us -> 94.4 us
  local copies, waits for them, and re-layouts: 2.79 us -> 0 us
    pallas_call x3 -> x2, Pallas kernels: 115 us -> 94.4 us  [the longest x1 92.7 us: shards(): pl.pallas_call(kernel, out_shape=[jax.ShapeDtypeStruct((WIDTH // 4, L), F...]
    unnamed x2 -> x0, local copies, waits for them, and re-layouts: 2.79 us -> none
where the time goes in v3:
time: 96.1 us; the launch traced here: 95 us
  Pallas kernels  94.4 us (98%)
    pallas_call x1, Pallas kernels, shards(): pl.pallas_call(kernel, out_shape=[jax.ShapeDtypeStruct((WIDTH // 4, L), F...  92.7 us

profile of v3, /device:TPU:6, one launch (start us, length us, event | category | flops | bytes accessed | tf_op | source)
XLA Modules:
  0.0 95.0 jit_solution(9646481741152582645)
XLA Ops:
  0.6 92.7 %shard_map.122 = (f32[512,128]{1,0:T(8,128)}, f32[1,128]{1,0:T(1,128)}) custom-call(s32[1,128]{1,0:T(1,128)} %bitcast.9, bf16[128,2048]{1,0:T(8,128)(2,1)} %residual.1, s32[1,2048]{1,0:T(1,128)} %bitcast.8, bf16[12,2048]{1,0:T(8,128)(2,1)} %embedding.1, bf16[2048,512]{1,0:T(8,128)(2,1)} %x_weight.1, bf16[2048,256]{1,0:T(8,128)(2,1)} %bc_weight.1, ...), custom_call_target="tpu_custom_call" | custom-call | tf_op jit(solution)/shard_map/pallas_call | solution.py:529
  93.3 1.7 %shard_map.123 = (f32[512,128]{1,0:T(8,128)}, f32[1,128]{1,0:T(1,128)}) custom-call(f32[512,128]{1,0:T(8,128)} %get-tuple-element.6.grad, f32[1,128]{1,0:T(1,128)} %get-tuple-element.7.saliency), custom_call_target="tpu_custom_call" | custom-call | tf_op jit(solution)/shard_map/pallas_call | solution.py:545

commit v4 on v3

--- a/solution.py
+++ b/solution.py
@@ -446,35 +446,46 @@
     slot = jnp.where(edge, 0, 1)
     total, weighed = chunk(3 - head)
     part[0] = total
-    give(part.at[0], got.at[slot], 0, slot, jnp.where(edge, near, 3 - head))
+    route = [
+        (part.at[0], got.at[slot], 0, slot, jnp.where(edge, near, 3 - head)),
+        (part.at[1], got.at[2], 1, 2, second),
+        (part.at[2], got.at[3], 2, 3, third),
+    ]
+    handover(*route[0]).start()
     total, share = chunk(second)
     weighed = weighed + share
     part[1] = total
-    give(part.at[1], got.at[2], 1, 2, second)
+
+    @pl.when(jnp.logical_not(edge))
+    def _():
+        handover(*route[1]).start()
+
     total, share = chunk(third)
     weighed = weighed + share
     part[2] = total
-
-    @pl.when(edge)
-    def _():
-        handover(part.at[2], got.at[3], 2, 3, third).start()
-
     total, share = chunk(head)
     weighed = weighed + share
     grad[...] = total
     sal_part[...] = jnp.broadcast_to(weighed, (8, L))
     sal_got[head] = sal_part[...]
-    scan_sends = list(started[:-2])
-    del started[:-2]
+    scan_sends = list(started)
+    del started[:]
     shares = [
         give(sal_part, sal_got.at[head], 2 + d, 3 + d, h_peer[d - 1][1]) for d in (1, 2, 3)
     ]
+
+    @pl.when(edge)
+    def _():
+        handover(*route[0]).wait_send()
+        handover(*route[1]).start()
+        handover(*route[2]).start()
 
     @pl.when(jnp.logical_not(edge))
     def _():
         arrived(0)
         part[2] = part[2] + got[0]
-        handover(part.at[2], got.at[3], 2, 3, third).start()
+        handover(*route[2]).start()
+        handover(*route[0]).wait_send()
 
     for copy in scan_sends:
         copy.wait_send()
@@ -493,7 +504,8 @@
     grad[...] = grad[...] + got[2]
     arrived(3)
     grad[...] = grad[...] + got[3]
-    handover(part.at[2], got.at[3], 2, 3, third).wait_send()
+    handover(*route[1]).wait_send()
+    handover(*route[2]).wait_send()
     for copy in started:
         copy.wait_send()
 

time: 96.1 us -> 96.1 us (level)
  no operation moved by 1% of the time
where the time goes in v4:
time: 96.1 us; the launch traced here: 95 us
  Pallas kernels  94.4 us (98%)
    pallas_call x1, Pallas kernels, shards(): pl.pallas_call(kernel, out_shape=[jax.ShapeDtypeStruct((WIDTH // 4, L), F...  92.7 us

profile of v4, /device:TPU:6, one launch (start us, length us, event | category | flops | bytes accessed | tf_op | source)
XLA Modules:
  0.0 95.0 jit_solution(7605108043589536974)
XLA Ops:
  0.6 92.7 %shard_map.122 = (f32[512,128]{1,0:T(8,128)}, f32[1,128]{1,0:T(1,128)}) custom-call(s32[1,128]{1,0:T(1,128)} %bitcast.9, bf16[128,2048]{1,0:T(8,128)(2,1)} %residual.1, s32[1,2048]{1,0:T(1,128)} %bitcast.8, bf16[12,2048]{1,0:T(8,128)(2,1)} %embedding.1, bf16[2048,512]{1,0:T(8,128)(2,1)} %x_weight.1, bf16[2048,256]{1,0:T(8,128)(2,1)} %bc_weight.1, ...), custom_call_target="tpu_custom_call" | custom-call | tf_op jit(solution)/shard_map/pallas_call | solution.py:541
  93.3 1.7 %shard_map.123 = (f32[512,128]{1,0:T(8,128)}, f32[1,128]{1,0:T(1,128)}) custom-call(f32[512,128]{1,0:T(8,128)} %get-tuple-element.6.grad, f32[1,128]{1,0:T(1,128)} %get-tuple-element.7.saliency), custom_call_target="tpu_custom_call" | custom-call | tf_op jit(solution)/shard_map/pallas_call | solution.py:557

commit v5 on v4

--- a/solution.py
+++ b/solution.py
@@ -151,9 +151,9 @@
 
 
 def kernel(
-    tokens, residual, pairing, embedding, x_weight, bc_weight, dt_rows, bias, rate, skip, cotangent,
+    tokens, residual_far, pairing, embedding, x_far, bc_far, dt_rows, bias, rate, skip, cotangent_far,
     grad, saliency,
-    source, layer_t, ups, x, mixed, zs, strides, runs, stride_e, decay_e, carried, grown,
+    residual, x_weight, bc_weight, cotangent, load, source, layer_t, ups, x, mixed, zs, strides, runs, stride_e, decay_e, carried, grown,
     g_x, g_mixed, g_read, g_write, x_paired, bc_paired, dt_paired,
     sums, factors, mate_in, mate_fac, chip, z_in, z_pre, x_in, y_in, e_out, e_in, far, far_in,
     x_fac, z_fac, states, d_x, d_mixed, d_pre, forward, part, got, sal_part, sal_got,
@@ -177,8 +177,16 @@
     y_peer = [device(other(yy, d), xx, z, core) for d in (1, 2, 3)]
     h_peer = [(seq, other(head, d)) for d in (1, 2, 3)]
     barrier = pltpu.get_barrier_semaphore()
-    for peer in [mate] + z_peer + x_peer + y_peer + h_peer:
+    for peer in z_peer + y_peer + x_peer + h_peer + [mate]:
         pl.semaphore_signal(barrier, inc=1, device_id=peer, device_id_type=MESH)
+    loads = [
+        pltpu.make_async_copy(source_ref, target, load.at[index])
+        for index, (source_ref, target) in enumerate((
+            (residual_far, residual), (x_far, x_weight), (bc_far, bc_weight), (cotangent_far, cotangent)
+        ))
+    ]
+    for copy in loads:
+        copy.start()
     started = []
 
     def push(source_ref, target, slot, peer):
@@ -370,7 +378,10 @@
             )
         return total + lax.dot_general(dt_cols, d_pre[branch], NT, preferred_element_type=F32)
 
+    loads[0].wait()
     layer = embed(tokens[...], embedding[...], residual[...])
+    for copy in loads[1:]:
+        copy.wait()
     ups[...] = cotangent[...].astype(F32)
     front(0, layer)
     pl.semaphore_wait(barrier, 13)
@@ -511,6 +522,7 @@
 
 
 VM = pl.BlockSpec(memory_space=pltpu.VMEM)
+AT = pl.BlockSpec(memory_space=pl.ANY)
 
 
 def final_kernel(grad, saliency, grad_out, saliency_out):
@@ -543,9 +555,13 @@
         out_shape=[
             jax.ShapeDtypeStruct((WIDTH // 4, L), F32), jax.ShapeDtypeStruct((1, L), F32),
         ],
-        in_specs=[VM] * 11,
+        in_specs=[AT if index in (1, 4, 5, 10) else VM for index in range(11)],
         out_specs=[VM] * 2,
-        scratch_shapes=[pltpu.VMEM(*shape) for shape in shapes]
+        scratch_shapes=[
+            pltpu.VMEM((L, WIDTH), BF16), pltpu.VMEM((WIDTH, HP), BF16),
+            pltpu.VMEM((WIDTH, 2 * N), BF16), pltpu.VMEM((L, HP), BF16), dma((4,)),
+        ]
+        + [pltpu.VMEM(*shape) for shape in shapes]
         + [dma((58,)), dma((58,)), dma((6,)), dma((7,))],
         compiler_params=pltpu.CompilerParams(
             collective_id=0, has_side_effects=True, vmem_limit_bytes=60 << 20

time: 96.1 us -> 96 us (level)
  no operation moved by 1% of the time
where the time goes in v5:
time: 96 us; the launch traced here: 94.3 us
  Pallas kernels  93.7 us (98%)
    pallas_call x1, Pallas kernels, shards(): pl.pallas_call(kernel, out_shape=[jax.ShapeDtypeStruct((WIDTH // 4, L), F...  92 us

profile of v5, /device:TPU:6, one launch (start us, length us, event | category | flops | bytes accessed | tf_op | source)
XLA Modules:
  0.0 94.3 jit_solution(7009547365023586873)
XLA Ops:
  0.6 92.0 %shard_map.122 = (f32[512,128]{1,0:T(8,128)}, f32[1,128]{1,0:T(1,128)}) custom-call(s32[1,128]{1,0:T(1,128)} %bitcast.9, bf16[128,2048]{1,0:T(8,128)(2,1)} %residual_far.1, s32[1,2048]{1,0:T(1,128)} %bitcast.8, bf16[12,2048]{1,0:T(8,128)(2,1)} %embedding.1, bf16[2048,512]{1,0:T(8,128)(2,1)} %x_far.1, bf16[2048,256]{1,0:T(8,128)(2,1)} %bc_far.1, ...), custom_call_target="tpu_custom_call" | custom-call | tf_op jit(solution)/shard_map/pallas_call | solution.py:553
  92.7 1.7 %shard_map.123 = (f32[512,128]{1,0:T(8,128)}, f32[1,128]{1,0:T(1,128)}) custom-call(f32[512,128]{1,0:T(8,128)} %get-tuple-element.6.grad, f32[1,128]{1,0:T(1,128)} %get-tuple-element.7.saliency), custom_call_target="tpu_custom_call" | custom-call | tf_op jit(solution)/shard_map/pallas_call | solution.py:573
